TPU v7x, 32 devices: a whole 2x2x4 slice. The times are simulated.
32 devices in a mesh: rows: 8 (over y, x, core), sub: 4 (over z).
Axes of the slice: x: 2, y: 2, z: 4, core: 2. Of those that a mesh axis runs over, the one named last changes fastest.
Arguments:
- old_basis: bfloat16 [32, 524288], P(None, ('rows', 'sub')), may hold values from -1 to 1
- snapshots: bfloat16 [512, 524288], P(None, ('rows', 'sub')), may hold values from -16 to 16
- gap_flags: int32 [512, 4096], P(None, ('rows', 'sub')), may hold values from 0 to 1, as said below
- sketch_seed: int32 [512, 64], replicated, may hold values from -1 to 1
Outputs:
- new_basis: float32 [32, 524288], P(None, ('rows', 'sub'))
- coefficients: float32 [32, 512], replicated
Inputs may be any that keep to these rules, and one draw needn't show every extreme that they name: `gap_flags`: 1 marks a block of 128 velocity rows measured in that snapshot, 0 a gap; every snapshot has measured blocks and gaps.
All inputs are finite; a program needn't handle non-finite values.
Results may differ from a plain program's by a relative error of at most 0.00135.
The roundings to bfloat16 on the way count: a program that leaves them out, or rounds other values in their place, can miss the bound.
Values may be sent and summed in bfloat16 or wider, within the bound.
No kernel may reach another device: no remote copies, remote signals or barrier semaphores. Data moves between devices by JAX's collectives and lax.ppermute only.
A program may use at most 192 MiB of HBM per device.

v0:
```python
import math

import jax
import jax.numpy as jnp
from jax import lax
from jax.sharding import PartitionSpec as P

POWER = 2


damping = 0.005
highest = lax.Precision.HIGHEST


def cholesky_last(system):
    extent = system.shape[0]
    factor = jnp.zeros_like(system)
    for column in range(extent):
        partial_sum = jnp.sum(factor * factor[column : column + 1], axis=1)
        remain = system[:, column] - partial_sum
        diagonal_root = jnp.sqrt(remain[column])
        lower_part = (jnp.arange(extent) >= column).reshape((extent,) + (1,) * (system.ndim - 2))
        factor = factor.at[:, column].set(jnp.where(lower_part, remain / diagonal_root, 0.0))
    return factor


def lower_solve(factor, target):
    extent = factor.shape[0]
    result = jnp.zeros_like(target)
    for column in range(extent):
        current = (target[column] - jnp.sum(factor[column] * result, axis=0)) / factor[
            column, column
        ]
        result = result.at[column].set(current)
    return result


def upper_solve(factor, target):
    extent = factor.shape[0]
    result = jnp.zeros_like(target)
    for column in reversed(range(extent)):
        current = (target[column] - jnp.sum(factor[:, column] * result, axis=0)) / factor[
            column, column
        ]
        result = result.at[column].set(current)
    return result


def solve_normal(grams, right, modes, rows_all):
    snapshot_count = grams.shape[0]
    identity = jnp.eye(modes, dtype=jnp.float32)[:, :, None]
    system = grams.T.reshape(modes, modes, snapshot_count) + damping * rows_all * identity
    factor = cholesky_last(system)
    return upper_solve(factor, lower_solve(factor, right.T))


def inverse_factor(products):
    extent = products.shape[0]
    factor = cholesky_last(products[:, :, None])
    return lower_solve(factor, jnp.eye(extent, dtype=jnp.float32))


def mask_blocks(samples, flag_blocks):
    snapshot_count, blocks_dev = flag_blocks.shape
    weights = flag_blocks.astype(samples.dtype)[:, :, None]
    return (samples.reshape(snapshot_count, blocks_dev, -1) * weights).reshape(snapshot_count, -1)


def refill(samples, flag_blocks, recon_low):
    snapshot_count, blocks_dev = flag_blocks.shape
    observed = (flag_blocks > 0)[:, :, None]
    combined = jnp.where(
        observed,
        samples.reshape(snapshot_count, blocks_dev, -1),
        recon_low.reshape(snapshot_count, blocks_dev, -1),
    )
    return combined.reshape(snapshot_count, -1)


def contract_rows(former, latter):
    return lax.dot_general(
        former, latter, (((1,), (1,)), ((), ())), preferred_element_type=jnp.float32
    )


def contract_first(former, latter):
    return lax.dot_general(
        former, latter, (((0,), (0,)), ((), ())), preferred_element_type=jnp.float32
    )


def per_device(old_basis, snapshots, gap_flags, sketch_seed):
    modes = old_basis.shape[0]
    rows_all = old_basis.shape[1] * lax.axis_size(("rows", "sub"))
    blocks_dev = gap_flags.shape[1]
    masked = mask_blocks(snapshots, gap_flags)
    right = contract_rows(masked, old_basis)
    pieces = old_basis.reshape(modes, blocks_dev, -1)
    block_grams = jnp.einsum("kbi,lbi->bkl", pieces, pieces, preferred_element_type=jnp.float32)
    block_rows = block_grams.reshape(blocks_dev, modes * modes)
    grams = jnp.dot(gap_flags.astype(jnp.float32), block_rows, precision=highest)
    mixer = sketch_seed.astype(jnp.bfloat16)
    gram_total, right_total = lax.psum((grams, right), ("rows", "sub"))
    coefficients = solve_normal(gram_total, right_total, modes, rows_all)
    recon_low = contract_first(coefficients.astype(jnp.bfloat16), old_basis).astype(jnp.bfloat16)
    filled = refill(snapshots, gap_flags, recon_low)
    sketch = contract_first(mixer, filled)
    inverse = None
    for sweep_index in range(POWER + 1):
        if sweep_index > 0:
            sketch = contract_first(mixer, filled)
        local_gram = lax.dot_general(
            sketch,
            sketch,
            (((1,), (1,)), ((), ())),
            precision=highest,
            preferred_element_type=jnp.float32,
        )
        products = lax.psum(local_gram, ("rows", "sub"))
        inverse = inverse_factor(products)
        if sweep_index < POWER:
            ortho_rows = jnp.dot(inverse, sketch, precision=highest).astype(jnp.bfloat16)
            mixer_share = lax.psum_scatter(
                contract_rows(filled, ortho_rows), ("rows", "sub"), scatter_dimension=0, tiled=True
            ).astype(jnp.bfloat16)
            mixer = lax.all_gather(mixer_share, ("rows", "sub"), axis=0, tiled=True)
    root_rows = math.sqrt(rows_all)
    new_basis = jnp.dot(inverse[:modes], sketch, precision=highest) * root_rows
    return (new_basis, coefficients)


def solution(mesh):
    in_specs = (P(None, ("rows", "sub")), P(None, ("rows", "sub")), P(None, ("rows", "sub")), P())
    out_specs = (P(None, ("rows", "sub")), P())
    return jax.shard_map(
        per_device, mesh=mesh, in_specs=in_specs, out_specs=out_specs, check_vma=False
    )
```

profile of v0, /device:TPU:0, one launch (start us, length us, event | category | flops | bytes accessed | tf_op | source)
XLA Modules:
  0.0 1549.9 jit_solution(17264317991794373059)
XLA Ops:
  9.1 2.1 copy.518
  11.2 2.8 fusion.6
  14.1 2.5 copy.519
  16.6 12.7 mul.4308
  29.3 24.4 %fusion.2 = f32[32,512]{1,0:T(8,128)} fusion(bf16[32,16384]{1,0:T(8,128)(2,1)S(1)} %copy-done, bf16[512,16384]{1,0:T(8,128)(2,1)} %param.965, bf16[64,8,128,128]{3,2,1,0:T(8,128)(2,1)} %bitcast.3922), kind=kOutput, calls=%fused_computation.40 | convolution fusion | flops 545259520 | bytes 34668544 | tf_op jit(solution)/shard_map/dot_general | solution.py:81
  54.5 137.0 %all-reduce.12.cloned.1.call-done = (f32[32,32,512]{2,0,1:T(8,128)}, f32[32,512]{1,0:T(8,128)}) async-done(((f32[32,32,512]{2,0,1:T(8,128)}, f32[32,512]{1,0:T(8,128)}), (f32[32,32,512]{2,0,1:T(8,128)}, f32[32,512]{1,0:T(8,128)})) %all-reduce.12.cloned.1.call-update) | async-done | bytes 2162704 | tf_op jit(solution)/shard_map/psum | solution.py:103
  191.5 1.8 broadcast_add_fusion
  291.4 12.0 broadcast_in_dim.635
  303.4 15.2 bitcast_select_fusion
  318.5 8.8 fusion.224
  327.3 1.9 copy-done.5
  329.3 3.4 convolution_bitcast_fusion.2
  332.7 39.6 %psum.37 = f32[64,64,1]{1,0,2:T(8,128)S(1)} all-reduce(f32[64,64,1]{1,0,2:T(8,128)S(1)} %convolution_bitcast_fusion.2), channel_id=1, replica_groups=mesh['rows'=8,'sub'=4] {'rows','sub'}, use_global_device_ids=true, to_apply=%region_97.98 | all-reduce | flops 4096 | bytes 32768 | tf_op jit(solution)/shard_map/psum | solution.py:119
  498.6 1.4 fusion.505
  500.0 1.4 fusion.504
  510.0 1.4 fusion.497
  515.8 1.4 fusion.493
  530.2 1.4 fusion.483
  537.4 1.4 fusion.478
  565.8 1.4 fusion.458
  578.6 1.4 fusion.449
  581.4 6.0 convolution_convert_fusion.2
  587.4 8.8 fusion.526
  596.3 133.9 %reduce-scatter.3.cloned.1.call-done = f32[16,64]{1,0:T(8,128)} async-done(((f32[512,64]{1,0:T(8,128)}), f32[16,64]{1,0:T(8,128)}) %reduce-scatter.3.cloned.1.call-update) | async-done | bytes 4112 | tf_op jit(solution)/shard_map/reduce_scatter | solution.py:123
  730.8 65.0 %all_gather.6 = bf16[512,64]{1,0:T(8,128)(2,1)S(1)} all-gather(bf16[16,64]{1,0:T(8,128)(2,1)S(1)} %convert_element_type.415), channel_id=1, replica_groups=mesh['rows'=8,'sub'=4] {'rows','sub'}, dimensions={0}, use_global_device_ids=true | all-gather | bytes 67584 | tf_op jit(solution)/shard_map/all_gather | solution.py:126
  795.8 8.9 fusion.527
  804.7 1.9 copy-done.4
  806.6 3.4 convolution_bitcast_fusion.1
  810.0 39.9 %psum.38 = f32[64,64,1]{1,0,2:T(8,128)S(1)} all-reduce(f32[64,64,1]{1,0,2:T(8,128)S(1)} %convolution_bitcast_fusion.1), channel_id=1, replica_groups=mesh['rows'=8,'sub'=4] {'rows','sub'}, use_global_device_ids=true, to_apply=%region_226.227 | all-reduce | flops 4096 | bytes 32768 | tf_op jit(solution)/shard_map/psum | solution.py:119
  970.9 1.9 subtract_divide_fusion.3
  972.9 1.4 fusion.447
  974.4 1.4 fusion.446
  980.1 1.4 fusion.442
  981.6 1.4 fusion.441
  991.6 1.4 fusion.434
  993.1 1.4 fusion.433
  997.4 1.4 fusion.430
  1011.7 1.4 fusion.420
  1019.0 1.4 fusion.415
  1047.4 1.4 fusion.395
  1060.1 1.4 fusion.386
  1063.0 6.0 convolution_convert_fusion.1
  1068.9 8.8 fusion.528
  1077.8 133.0 %reduce-scatter.5.cloned.1.call-done = f32[16,64]{1,0:T(8,128)} async-done(((f32[512,64]{1,0:T(8,128)}), f32[16,64]{1,0:T(8,128)}) %reduce-scatter.5.cloned.1.call-update) | async-done | bytes 4112 | tf_op jit(solution)/shard_map/reduce_scatter | solution.py:123
  1211.5 65.0 %all_gather.7 = bf16[512,64]{1,0:T(8,128)(2,1)S(1)} all-gather(bf16[16,64]{1,0:T(8,128)(2,1)S(1)} %convert_element_type.417), channel_id=1, replica_groups=mesh['rows'=8,'sub'=4] {'rows','sub'}, dimensions={0}, use_global_device_ids=true | all-gather | bytes 67584 | tf_op jit(solution)/shard_map/all_gather | solution.py:126
  1276.4 8.9 fusion.529
  1285.4 1.9 copy-done.3
  1287.3 3.4 convolution_bitcast_fusion
  1290.7 39.9 %psum.39 = f32[64,64,1]{1,0,2:T(8,128)S(1)} all-reduce(f32[64,64,1]{1,0,2:T(8,128)S(1)} %convolution_bitcast_fusion), channel_id=1, replica_groups=mesh['rows'=8,'sub'=4] {'rows','sub'}, use_global_device_ids=true, to_apply=%region_355.356 | all-reduce | flops 4096 | bytes 32768 | tf_op jit(solution)/shard_map/psum | solution.py:119
  1451.0 1.9 subtract_divide_fusion.2
  1453.0 1.4 fusion.384
  1455.9 1.4 fusion.382
  1463.1 1.4 fusion.377
  1467.4 1.4 fusion.374
  1468.9 1.4 fusion.373
  1471.8 1.4 fusion.371
  1483.2 1.4 fusion.363
  1484.7 1.4 fusion.362
  1498.9 1.4 fusion.352
  1509.0 1.4 fusion.345
  1520.5 1.4 fusion.337
  1530.4 1.4 fusion.330
  1533.3 1.4 fusion.328
  1537.5 5.7 convolution_multiply_fusion
  (2302 shorter events, 542.9 us)
Async XLA Ops:
  7.2 1.3 copy-start
  7.2 184.3 %all-reduce.12.cloned.1.call-start = ((), (), s32[]{:S(2)}) async-start(), calls=%async_computation.4 | async-start | bytes 4325376 | tf_op jit(solution)/shard_map/psum | solution.py:103
  9.1 2.1 copy-start.8
  53.7 676.4 %reduce-scatter.3.cloned.1.call-start = ((), (), s32[]{:S(2)}) async-start(), calls=%async_computation.2 | async-start | bytes 270336 | tf_op jit(solution)/shard_map/reduce_scatter | solution.py:123
  54.4 443.4 %copy-start.9 = (f32[64,64]{1,0:T(8,128)}, f32[64,64]{1,0:T(8,128)S(1)}, u32[]{:S(2)}) copy-start(f32[64,64]{1,0:T(8,128)S(1)} %fusion.228) | copy-start | bytes 49156
  210.2 2.8 copy-start.2
  238.3 3.3 copy-start.6
  291.4 12.0 copy-start.7
  303.4 15.2 copy-start.10
  327.3 1.9 copy-start.5
  596.2 614.6 %reduce-scatter.5.cloned.1.call-start = ((), (), s32[]{:S(2)}) async-start(), calls=%async_computation.3 | async-start | bytes 270336 | tf_op jit(solution)/shard_map/reduce_scatter | solution.py:123
  804.7 1.9 copy-start.4
  1285.4 1.9 copy-start.3
  1537.4 5.7 copy-start.1
Sparse Core Ops, SparseCore 0:
  53.8 137.5 all-reduce.11
  596.3 133.7 reduce-scatter.2
  1077.9 132.8 reduce-scatter.4
where the time goes:
time: 1580 us; the launch traced here: 1550 us
  waiting for transfers between devices  404 us (26%)
  other arithmetic  393 us (25%)
  blocking collectives  249 us (16%)
  local copies, waits for them, and re-layouts  234 us (15%)
  between operations  155 us (10%)
  matrix products  115 us (7%)
    div x219, other arithmetic, lower_solve(): (target[column] - jnp.sum(factor[column] * result, axis=0)) / factor[colu...  267 us
    reduce_scatter x2, waiting for transfers between devices, per_device(): lax.psum_scatter(contract_rows(filled, ortho_rows), ('rows', 'sub'), scat...  267 us
    psum x1, waiting for transfers between devices, per_device(): gram_total, right_total = lax.psum((grams, right), ('rows', 'sub'))  137 us
    all_gather x2, blocking collectives, per_device(): mixer = lax.all_gather(mixer_share, ('rows', 'sub'), axis=0, tiled=True)  130 us
    psum x3, blocking collectives, per_device(): products = lax.psum(local_gram, ('rows', 'sub'))  119 us
    slice x192, local copies, waits for them, and re-layouts, cholesky_last(): diagonal_root = jnp.sqrt(remain[column])  113 us
    dot_general x3, matrix products, contract_rows(): lax.dot_general(former, latter, (((1,), (1,)), ((), ())), preferred_eleme...  42 us
    dot_general x4, matrix products, contract_first(): lax.dot_general(former, latter, (((0,), (0,)), ((), ())), preferred_eleme...  41.8 us
  transfers between devices with their start and end apart: 3, of which 3 were waited for; matrix products, arithmetic and copies ran while one was open for 0% of the time, Pallas kernels for 0%

commit v1 on v0

v1 whole, which is shorter than its diff:
```python
import functools
import math

import jax
import jax.numpy as jnp
from jax import lax
from jax.experimental import pallas as pl
from jax.experimental.pallas import tpu as pltpu
from jax.sharding import PartitionSpec as P

POWER = 2
DAMPING = 0.005
AXES = ("rows", "sub")
LANES = 128
HIGHEST = lax.Precision.HIGHEST
F32 = jnp.float32
BF16 = jnp.bfloat16

CONTRACT_LANES = (((1,), (1,)), ((), ()))


def dot_nt(left, right, precision=None):
    return lax.dot_general(
        left, right, CONTRACT_LANES, precision=precision, preferred_element_type=F32
    )


def dot_nn(left, right, precision=None):
    return jnp.dot(left, right, precision=precision, preferred_element_type=F32)


def split_three(values):
    first = values.astype(BF16)
    rest = values - first.astype(F32)
    second = rest.astype(BF16)
    third = (rest - second.astype(F32)).astype(BF16)
    return first, second, third


def flag_columns(flags_ref, blocks_step):
    shift = (LANES - pl.program_id(0) * blocks_step) % LANES
    return pltpu.roll(flags_ref[...].astype(F32), shift, 1).astype(BF16)


def normal_kernel(blocks_step, flags_ref, snap_ref, basis_ref, out_ref, gram_ref, right_ref):
    step = pl.program_id(0)
    count = flags_ref.shape[0]
    modes = basis_ref.shape[0]
    half = modes // 2
    columns = flag_columns(flags_ref, blocks_step)

    @pl.when(step == 0)
    def _():
        right_ref[...] = jnp.zeros_like(right_ref)

    masked = []
    for block in range(blocks_step):
        part = pl.ds(block * LANES, LANES)
        weight = jnp.broadcast_to(columns[:, block : block + 1], (count, LANES))
        masked.append(snap_ref[:, part] * weight)
        piece = basis_ref[:, part]
        copies = jnp.concatenate([piece] * (LANES // modes), axis=0)
        row = pl.multiple_of((step * blocks_step + block) * modes, modes)
        gram_ref[pl.ds(row, modes), :] = dot_nt(piece, copies)
    right_ref[...] += dot_nt(jnp.concatenate(masked, axis=1), basis_ref[...])

    @pl.when(step == pl.num_programs(0) - 1)
    def _():
        lane = lax.broadcasted_iota(jnp.int32, (LANES, LANES), 1)
        group = LANES // half
        tiles = []
        middle = jnp.zeros((LANES, LANES), F32)
        for tile_index in range(modes // group):
            tile = jnp.zeros((LANES, LANES), F32)
            for inner in range(group):
                mode = tile_index * group + inner
                rows = gram_ref[pl.ds(mode, LANES, stride=modes), :]
                moved = pltpu.roll(rows, (half * inner - mode) % LANES, 1)
                tile = jnp.where(lane // half == inner, moved, tile)
                if mode < half:
                    middle = jnp.where(lane == mode + half, rows, middle)
            tiles.append(tile)
        tiles.append(middle)
        block_rows = jnp.concatenate(tiles, axis=1)
        flags = flags_ref[...].astype(BF16)
        total = sum(dot_nn(flags, part) for part in split_three(block_rows))
        wide = tiles[0].shape[1] * (len(tiles) - 1)
        out_ref[:, :wide] = total[:, :wide]
        right = jnp.concatenate(
            [
                jnp.zeros((count, modes), F32),
                right_ref[...],
                jnp.zeros((count, LANES - 2 * modes), F32),
            ],
            axis=1,
        )
        out_ref[:, wide:] = total[:, wide:] + right


def normal_terms(flags, snapshots, basis, chunk=2048):
    count, rows = snapshots.shape
    modes = basis.shape[0]
    blocks = flags.shape[1]
    width = modes * modes // 2 + LANES
    return pl.pallas_call(
        functools.partial(normal_kernel, chunk // LANES),
        grid=(rows // chunk,),
        in_specs=[
            pl.BlockSpec((count, blocks), lambda i: (0, 0)),
            pl.BlockSpec((count, chunk), lambda i: (0, i)),
            pl.BlockSpec((modes, chunk), lambda i: (0, i)),
        ],
        out_specs=pl.BlockSpec((count, width), lambda i: (0, 0)),
        out_shape=jax.ShapeDtypeStruct((count, width), F32),
        scratch_shapes=[
            pltpu.VMEM((blocks * modes, LANES), F32),
            pltpu.VMEM((count, modes), F32),
        ],
        compiler_params=pltpu.CompilerParams(vmem_limit_bytes=48 << 20),
        name="normal_terms",
    )(flags, snapshots, basis)


def solve_kernel(modes, shift, in_ref, out_ref, turned_ref, system_ref):
    half = modes // 2
    count, width = in_ref.shape
    padded = jnp.concatenate([in_ref[...], jnp.zeros((LANES - count, width), F32)], axis=0)
    turned_ref[...] = padded.T
    for mode in range(modes):
        first = min(half, modes - mode)
        base = mode * half
        start = mode * modes + mode
        values = turned_ref[base : base + first, :]
        system_ref[start : start + first, :] = values
        if first < half:
            wrapped = turned_ref[base + first : base + half, :]
            system_ref[pl.ds(mode, half - first, stride=modes), :] = wrapped
    middle = modes * half + half
    system_ref[pl.ds(half, half, stride=modes + 1), :] = turned_ref[middle : middle + half, :]
    right = turned_ref[modes * half + modes : modes * half + 2 * modes, :]
    index = lax.broadcasted_iota(jnp.int32, (modes, LANES), 0)

    rows = [system_ref[k * modes : (k + 1) * modes, :] for k in range(modes)]
    scaled = []
    targets = []
    for column in range(modes):
        row = jnp.where(index == column, rows[column] + shift, rows[column])
        inverse = 1.0 / row[column : column + 1, :]
        factor = jnp.where(index > column, row * inverse, 0.0)
        target = right[column : column + 1, :]
        scaled.append(factor)
        targets.append(target * inverse)
        right = right - factor * target
        for k in range(column + 1, modes):
            rows[k] = rows[k] - factor[k : k + 1, :] * row
    result = jnp.zeros((modes, LANES), F32)
    for column in reversed(range(modes)):
        value = targets[column] - jnp.sum(scaled[column] * result, axis=0, keepdims=True)
        result = jnp.where(index == column, value, result)
    square = jnp.concatenate([result, jnp.zeros((LANES - modes, LANES), F32)], axis=0)
    out_ref[...] = square.T[:count, :modes]


def solve_share(share, modes, rows_all):
    count, width = share.shape
    return pl.pallas_call(
        functools.partial(solve_kernel, modes, DAMPING * rows_all),
        out_shape=jax.ShapeDtypeStruct((count, modes), F32),
        scratch_shapes=[
            pltpu.VMEM((width, LANES), F32),
            pltpu.VMEM((modes * modes, LANES), F32),
        ],
        name="solve_share",
    )(share)


def packed_blocks(tiles):
    return [(i, (i + d) % tiles) for d in range(tiles // 2) for i in range(tiles)] + [
        (i, i + tiles // 2) for i in range(tiles // 2)
    ]


def refill_kernel(
    blocks_step, flags_ref, snap_ref, basis_ref, coef_ref, fill_ref, corr_ref, sum_ref
):
    step = pl.program_id(0)
    count = flags_ref.shape[0]
    columns = flag_columns(flags_ref, blocks_step)
    coef = coef_ref[...].astype(BF16)

    @pl.when(step == 0)
    def _():
        sum_ref[...] = jnp.zeros_like(sum_ref)

    recon = dot_nn(coef, basis_ref[...]).astype(BF16)
    for block in range(blocks_step):
        part = pl.ds(block * LANES, LANES)
        weight = jnp.broadcast_to(columns[:, block : block + 1], (count, LANES))
        fill_ref[:, part] = jnp.where(
            weight > 0, snap_ref[:, part], recon[:, block * LANES : (block + 1) * LANES]
        )
    side = count // 2
    upper, lower = fill_ref[:side, :], fill_ref[side:, :]
    sum_ref[:side, :side] += dot_nt(upper, upper)
    sum_ref[:side, side:] += dot_nt(upper, lower)
    sum_ref[side:, side:] += dot_nt(lower, lower)

    @pl.when(step == pl.num_programs(0) - 1)
    def _():
        for place, (i, j) in enumerate(packed_blocks(count // LANES)):
            i, j = min(i, j), max(i, j)
            corr_ref[place * LANES : (place + 1) * LANES, :] = sum_ref[
                i * LANES : (i + 1) * LANES, j * LANES : (j + 1) * LANES
            ]


def refill_correlate(flags, snapshots, basis, coefs, chunk=2048):
    count, rows = snapshots.shape
    modes = basis.shape[0]
    blocks = flags.shape[1]
    packed = len(packed_blocks(count // LANES)) * LANES
    return pl.pallas_call(
        functools.partial(refill_kernel, chunk // LANES),
        grid=(rows // chunk,),
        in_specs=[
            pl.BlockSpec((count, blocks), lambda i: (0, 0)),
            pl.BlockSpec((count, chunk), lambda i: (0, i)),
            pl.BlockSpec((modes, chunk), lambda i: (0, i)),
            pl.BlockSpec((count, modes), lambda i: (0, 0)),
        ],
        out_specs=[
            pl.BlockSpec((count, chunk), lambda i: (0, i)),
            pl.BlockSpec((packed, LANES), lambda i: (0, 0)),
        ],
        out_shape=[
            jax.ShapeDtypeStruct((count, rows), BF16),
            jax.ShapeDtypeStruct((packed, LANES), F32),
        ],
        scratch_shapes=[pltpu.VMEM((count, count), F32)],
        compiler_params=pltpu.CompilerParams(vmem_limit_bytes=48 << 20),
        name="refill_correlate",
    )(flags, snapshots, basis, coefs)


def inverse_cholesky(products):
    extent = products.shape[0]
    row_index = lax.broadcasted_iota(jnp.int32, (extent, 2 * extent), 0)
    lane_index = lax.broadcasted_iota(jnp.int32, (extent, 2 * extent), 1)
    eye = jnp.where(
        lax.broadcasted_iota(jnp.int32, (extent, extent), 0)
        == lax.broadcasted_iota(jnp.int32, (extent, extent), 1),
        1.0,
        0.0,
    )
    work = jnp.concatenate([products, eye], axis=1)
    for column in range(extent - 1):
        row = work[column : column + 1, :]
        factor = work[:, column : column + 1] / row[:, column : column + 1]
        factor = jnp.broadcast_to(factor, work.shape)
        work = work - jnp.where(row_index > column, factor * row, 0.0)
    pivots = jnp.sum(jnp.where(row_index == lane_index, work, 0.0), axis=1, keepdims=True)
    return work[:, extent:] * (1.0 / jnp.sqrt(pivots))


def sweep_weights(mixer, full, rows):
    spread = dot_nn(mixer, full, HIGHEST)
    products = dot_nt(spread, mixer, HIGHEST)
    return dot_nn(inverse_cholesky(products)[:rows], mixer, HIGHEST)


def first_kernel(corr_ref, seed_ref, out_ref, full_ref):
    count = full_ref.shape[0]
    for place, (i, j) in enumerate(packed_blocks(count // LANES)):
        i, j = min(i, j), max(i, j)
        tile = corr_ref[place * LANES : (place + 1) * LANES, :]
        rows, cols = pl.ds(i * LANES, LANES), pl.ds(j * LANES, LANES)
        full_ref[rows, cols] = tile
        if i != j:
            full_ref[cols, rows] = tile.T
    mixer = seed_ref[...].astype(F32).T
    store_parts(out_ref, sweep_weights(mixer, full_ref[...], mixer.shape[0]))


def later_kernel(scale, full_ref, mixer_ref, out_ref):
    mixer = mixer_ref[...].astype(BF16).astype(F32)
    store_parts(out_ref, sweep_weights(mixer, full_ref[...], out_ref.shape[0] // 3) * scale)


def store_parts(out_ref, values):
    rows = values.shape[0]
    for place, part in enumerate(split_three(values)):
        out_ref[place * rows : (place + 1) * rows, :] = part


def first_weights(corr, seed):
    count, width = seed.shape
    return pl.pallas_call(
        first_kernel,
        out_shape=[
            jax.ShapeDtypeStruct((3 * width, count), BF16),
            jax.ShapeDtypeStruct((count, count), F32),
        ],
        name="first_weights",
    )(corr, seed)


def later_weights(full, mixer, rows, scale):
    return pl.pallas_call(
        functools.partial(later_kernel, scale),
        out_shape=jax.ShapeDtypeStruct((3 * rows, mixer.shape[1]), BF16),
        name="later_weights",
    )(full, mixer)


def mixer_kernel(weights_ref, fill_ref, out_ref):
    width = out_ref.shape[0]

    @pl.when(pl.program_id(0) == 0)
    def _():
        out_ref[...] = jnp.zeros_like(out_ref)

    terms = dot_nn(weights_ref[...], fill_ref[...])
    ortho = terms[:width] + (terms[width : 2 * width] + terms[2 * width :])
    out_ref[...] += dot_nt(ortho.astype(BF16), fill_ref[...])


def next_mixer(weights, filled, chunk=2048):
    count, rows = filled.shape
    width = weights.shape[0] // 3
    return pl.pallas_call(
        mixer_kernel,
        grid=(rows // chunk,),
        in_specs=[
            pl.BlockSpec(weights.shape, lambda i: (0, 0)),
            pl.BlockSpec((count, chunk), lambda i: (0, i)),
        ],
        out_specs=pl.BlockSpec((width, count), lambda i: (0, 0)),
        out_shape=jax.ShapeDtypeStruct((width, count), F32),
        compiler_params=pltpu.CompilerParams(vmem_limit_bytes=48 << 20),
        name="next_mixer",
    )(weights, filled)


def basis_kernel(weights_ref, fill_ref, out_ref):
    modes = out_ref.shape[0]
    terms = dot_nn(weights_ref[...], fill_ref[...])
    out_ref[...] = terms[:modes] + (terms[modes : 2 * modes] + terms[2 * modes :])


def project_basis(weights, filled, chunk=2048):
    count, rows = filled.shape
    modes = weights.shape[0] // 3
    return pl.pallas_call(
        basis_kernel,
        grid=(rows // chunk,),
        in_specs=[
            pl.BlockSpec(weights.shape, lambda i: (0, 0)),
            pl.BlockSpec((count, chunk), lambda i: (0, i)),
        ],
        out_specs=pl.BlockSpec((modes, chunk), lambda i: (0, i)),
        out_shape=jax.ShapeDtypeStruct((modes, rows), F32),
        compiler_params=pltpu.CompilerParams(vmem_limit_bytes=48 << 20),
        name="project_basis",
    )(weights, filled)


class Stage:
    def __init__(self, axis, size, bits):
        self.axis = axis
        self.pairs = [(i, i ^ (1 << bits[i & 1])) for i in range(size)]
        self.bits = bits

    def bit(self):
        place = lax.axis_index(self.axis)
        if self.bits[0] == self.bits[1]:
            return (place >> self.bits[0]) & 1
        return jnp.where(place & 1, place >> self.bits[1], place >> self.bits[0]) & 1

    def swap(self, values):
        return lax.ppermute(values, self.axis, self.pairs)


def stages():
    rows, sub = (lax.axis_size(name) for name in AXES)
    high = list(range(1, rows.bit_length() - 1))
    plan = [Stage("rows", rows, (0, 0))]
    plan += [Stage("rows", rows, bits) for bits in zip(high, reversed(high))]
    plan += [Stage("sub", sub, (bit, bit)) for bit in range(sub.bit_length() - 1)]
    return plan


def halve(values, stage):
    bit = stage.bit()
    half = values.shape[0] // 2
    keep = lax.dynamic_slice_in_dim(values, bit * half, half, 0)
    send = lax.dynamic_slice_in_dim(values, (1 - bit) * half, half, 0)
    return keep + stage.swap(send)


def join(values, stage):
    other = stage.swap(values)
    low = stage.bit() == 0
    return jnp.concatenate(
        [jnp.where(low, values, other), jnp.where(low, other, values)], axis=0
    )


def scatter_sum(values):
    for stage in stages():
        values = halve(values, stage)
    return values


def gather_shares(share):
    rows, sub = (lax.axis_size(name) for name in AXES)
    total = rows * sub
    spread = jnp.broadcast_to(share[None], (total, *share.shape))
    spread = lax.all_to_all(spread, AXES, 0, 0, tiled=True)
    high = rows.bit_length() - 2
    low = sub.bit_length() - 1
    cube = spread.reshape((2,) * high + (2,) + (2,) * low + share.shape)
    tail = high + low
    subs = [high + low - 1 - k for k in range(low)]
    sides = []
    for core in range(2):
        side = lax.index_in_dim(cube, core, high, keepdims=False)
        order = list(range(high)) if core else list(reversed(range(high)))
        sides.append(side.transpose(order + subs + [tail, tail + 1]))
    return jnp.stack(sides).reshape(total * share.shape[0], share.shape[1])


def sum_everywhere(values, halvings):
    plan = stages()
    for stage in plan[:halvings]:
        values = halve(values, stage)
    for stage in plan[halvings:]:
        values = values + stage.swap(values)
    for stage in reversed(plan[:halvings]):
        values = join(values, stage)
    return values


def per_device(old_basis, snapshots, gap_flags, sketch_seed):
    modes = old_basis.shape[0]
    rows_all = old_basis.shape[1] * lax.axis_size(AXES)
    terms = normal_terms(gap_flags, snapshots, old_basis)
    share = solve_share(scatter_sum(terms), modes, rows_all)
    coefs = gather_shares(share)
    filled, corr = refill_correlate(gap_flags, snapshots, old_basis, coefs)
    weights, full = first_weights(sum_everywhere(corr, 2), sketch_seed)
    width = sketch_seed.shape[1]
    for sweep in range(1, POWER + 1):
        mixer = sum_everywhere(next_mixer(weights, filled), 1)
        last = sweep == POWER
        rows = modes if last else width
        weights = later_weights(full, mixer, rows, math.sqrt(rows_all) if last else 1.0)
    return project_basis(weights, filled), coefs.T


def solution(mesh):
    split = P(None, AXES)
    return jax.shard_map(
        per_device,
        mesh=mesh,
        in_specs=(split, split, split, P()),
        out_specs=(split, P()),
        check_vma=False,
    )
```

time: 1580 us -> 223 us (0.14); the launches traced: 1550 us -> 222 us
  other arithmetic: 393 us -> 4.14 us
  waiting for transfers between devices: 404 us -> 88.5 us
  blocking collectives: 249 us -> 0 us
  local copies, waits for them, and re-layouts: 234 us -> 8.91 us
  between operations: 155 us -> 1.02 us
  matrix products: 115 us -> 0 us
  Pallas kernels: 0 us -> 94.9 us
  starting transfers between devices: 0.37 us -> 24.7 us
    div x255 -> x0, other arithmetic: 291 us -> none  [the longest x219 267 us: lower_solve(): (target[column] - jnp.sum(factor[column] * result, axis=0)) / factor[colu...]
    reduce_scatter x2 -> x0, waiting for transfers between devices: 267 us -> none  [per_device(): lax.psum_scatter(contract_rows(filled, ortho_rows), ('rows', 'sub'), scat...]
    psum x1 -> x0, waiting for transfers between devices: 137 us -> none  [per_device(): gram_total, right_total = lax.psum((grams, right), ('rows', 'sub'))]
    slice x247 -> x1, local copies, waits for them, and re-layouts: 131 us -> 0.02 us  [gather_shares(): side = lax.index_in_dim(cube, core, high, keepdims=False)]
    all_gather x2 -> x0, blocking collectives: 130 us -> none  [per_device(): mixer = lax.all_gather(mixer_share, ('rows', 'sub'), axis=0, tiled=True)]
    psum x3 -> x0, blocking collectives: 119 us -> none  [per_device(): products = lax.psum(local_gram, ('rows', 'sub'))]
    dot_general x15 -> x0, matrix products: 115 us -> none  [the longest x3 42 us: contract_rows(): lax.dot_general(former, latter, (((1,), (1,)), ((), ())), preferred_eleme...]
    pallas_call x0 -> x9, Pallas kernels: none -> 94.9 us  [the longest x2 25.1 us: next_mixer(): pl.pallas_call(mixer_kernel, grid=(rows // chunk,), in_specs=[pl.BlockSpe...]
  transfers between devices with their start and end apart: 3 -> 25, of which waited for: 3 -> 25; matrix products, arithmetic and copies ran while one was open for 0% -> 1% of each run, Pallas kernels for 0% -> 0%
where the time goes in v1:
time: 223 us; the launch traced here: 222 us
  Pallas kernels  94.9 us (43%)
  waiting for transfers between devices  88.5 us (40%)
  starting transfers between devices  24.7 us (11%)
  local copies, waits for them, and re-layouts  8.91 us (4%)
  other arithmetic  4.14 us (2%)
    ppermute x24, waiting for transfers between devices, swap(): return lax.ppermute(values, self.axis, self.pairs)  81.2 us
    pallas_call x2, Pallas kernels, next_mixer(): pl.pallas_call(mixer_kernel, grid=(rows // chunk,), in_specs=[pl.BlockSpe...  25.1 us
    pallas_call x1, Pallas kernels, refill_correlate(): pl.pallas_call(functools.partial(refill_kernel, chunk // LANES), grid=(ro...  20 us
    ppermute x24, starting transfers between devices, swap(): return lax.ppermute(values, self.axis, self.pairs)  18 us
    pallas_call x2, Pallas kernels, later_weights(): pl.pallas_call(functools.partial(later_kernel, scale), out_shape=jax.Shap...  14.3 us
    pallas_call x1, Pallas kernels, normal_terms(): pl.pallas_call(functools.partial(normal_kernel, chunk // LANES), grid=(ro...  13.9 us
    pallas_call x1, Pallas kernels, project_basis(): pl.pallas_call(basis_kernel, grid=(rows // chunk,), in_specs=[pl.BlockSpe...  10.4 us
    pallas_call x1, Pallas kernels, first_weights(): pl.pallas_call(first_kernel, out_shape=[jax.ShapeDtypeStruct((3 * width,...  8.63 us
  transfers between devices with their start and end apart: 25, of which 25 were waited for; matrix products, arithmetic and copies ran while one was open for 1% of the time, Pallas kernels for 0%

profile of v1, /device:TPU:0, one launch (start us, length us, event | category | flops | bytes accessed | tf_op | source)
XLA Modules:
  0.0 222.2 jit_solution(12358844914468334551)
XLA Ops:
  0.6 1.2 copy-done
  1.9 0.9 copy-done.2
  2.8 13.9 %normal_terms.1 = f32[512,640]{1,0:T(8,128)S(1)} custom-call(s32[512,128]{1,0:T(8,128)S(1)} %copy-done.2, bf16[512,16384]{1,0:T(8,128)(2,1)} %snap_ref.3, bf16[32,16384]{1,0:T(8,128)(2,1)S(1)} %copy-done), custom_call_target="tpu_custom_call" | custom-call | tf_op jit(solution)/shard_map/normal_terms/pallas_call | solution.py:105
  16.8 0.5 collective-permute-start
  17.4 1.7 collective-permute-done
  19.2 2.9 %collective-permute-start.1 = (f32[128,640]{1,0:T(8,128)S(1)}, f32[128,640]{1,0:T(8,128)S(1)}, u32[]{:S(2)}, u32[]{:S(2)}) collective-permute-start(f32[128,640]{1,0:T(8,128)S(1)} %constant_dynamic-slice_fusion.7), channel_id=1, source_target_pairs={{0,8},{4,20},{8,0},{12,28},{16,24},{20,4},{24,16},{28,12},{1,9},{5... | collective-permute-start | bytes 983048 | tf_op jit(solution)/shard_map/ppermute | solution.py:380
  22.1 5.1 %collective-permute-done.1 = f32[128,640]{1,0:T(8,128)S(1)} collective-permute-done((f32[128,640]{1,0:T(8,128)S(1)}, f32[128,640]{1,0:T(8,128)S(1)}, u32[]{:S(2)}, u32[]{:S(2)}) %collective-permute-start.1) | collective-permute-done | bytes 327712 | tf_op jit(solution)/shard_map/ppermute | solution.py:380
  27.2 2.1 collective-permute-start.2
  29.4 3.3 %collective-permute-done.2 = f32[64,640]{1,0:T(8,128)S(1)} collective-permute-done((f32[64,640]{1,0:T(8,128)S(1)}, f32[64,640]{1,0:T(8,128)S(1)}, u32[]{:S(2)}, u32[]{:S(2)}) %collective-permute-start.2) | collective-permute-done | bytes 163872 | tf_op jit(solution)/shard_map/ppermute | solution.py:380
  32.7 2.1 collective-permute-start.3
  34.8 2.4 %collective-permute-done.3 = f32[32,640]{1,0:T(8,128)S(1)} collective-permute-done((f32[32,640]{1,0:T(8,128)S(1)}, f32[32,640]{1,0:T(8,128)S(1)}, u32[]{:S(2)}, u32[]{:S(2)}) %collective-permute-start.3) | collective-permute-done | bytes 81952 | tf_op jit(solution)/shard_map/ppermute | solution.py:380
  37.3 3.3 %collective-permute-start.4 = (f32[16,640]{1,0:T(8,128)S(1)}, f32[16,640]{1,0:T(8,128)S(1)}, u32[]{:S(2)}, u32[]{:S(2)}) collective-permute-start(f32[16,640]{1,0:T(8,128)S(1)} %constant_dynamic-slice_fusion.4), channel_id=1, source_target_pairs={{0,2},{1,3},{2,0},{3,1},{4,6},{5,7},{6,4},{7,5},{8,10},{9,11},{10,... | collective-permute-start | bytes 122888 | tf_op jit(solution)/shard_map/ppermute | solution.py:380
  40.6 2.0 collective-permute-done.4
  42.6 0.6 dynamic-slice_add_fusion.8.in_ref
  43.2 2.6 %solve_share.1 = f32[16,32]{1,0:T(8,128)} custom-call(f32[16,640]{1,0:T(8,128)} %dynamic-slice_add_fusion.8.in_ref), custom_call_target="tpu_custom_call" | custom-call | tf_op jit(solution)/shard_map/solve_share/pallas_call | solution.py:166
  45.7 0.7 broadcast_in_dim.2
  46.5 0.8 reshape.13
  47.3 6.6 %all-to-all-start = ((f32[32,1,512]{2,1,0:T(1,128)}), f32[32,1,512]{2,1,0:T(1,128)S(1)}, u32[]{:S(2)}, u32[]{:S(2)}) async-start(f32[32,1,512]{2,1,0:T(1,128)} %reshape.13), calls=%async_computation | async-start | bytes 131072 | tf_op jit(solution)/shard_map/all_to_all | solution.py:418
  53.9 7.3 %all-to-all-done = f32[32,1,512]{2,1,0:T(1,128)S(1)} async-done(((f32[32,1,512]{2,1,0:T(1,128)}), f32[32,1,512]{2,1,0:T(1,128)S(1)}, u32[]{:S(2)}, u32[]{:S(2)}) %all-to-all-start) | async-done | bytes 65568 | tf_op jit(solution)/shard_map/all_to_all | solution.py:418
  61.2 0.5 broadcast.1
  61.7 0.8 reduce
  62.8 20.0 %refill_correlate.1 = (bf16[512,16384]{1,0:T(8,128)(2,1)}, f32[1280,128]{1,0:T(8,128)S(1)}) custom-call(s32[512,128]{1,0:T(8,128)S(1)} %copy-done.3, bf16[512,16384]{1,0:T(8,128)(2,1)} %snap_ref.3, bf16[32,16384]{1,0:T(8,128)(2,1)S(1)} %copy-done.1, f32[512,32]{1,0:T(8,128)S(1)} %bitcast.17), custom_call_target="tpu_custom_call" | custom-call | tf_op jit(solution)/shard_map/refill_correlate/pallas_call | solution.py:222
  82.9 1.6 collective-permute-done.5
  84.5 0.7 collective-permute-start.6
  85.3 4.7 %collective-permute-done.6 = f32[320,128]{1,0:T(8,128)S(1)} collective-permute-done((f32[320,128]{1,0:T(8,128)S(1)}, f32[320,128]{1,0:T(8,128)S(1)}, u32[]{:S(2)}, u32[]{:S(2)}) %collective-permute-start.6) | collective-permute-done | bytes 163872 | tf_op jit(solution)/shard_map/ppermute | solution.py:380
  89.9 0.7 collective-permute-start.7
  90.7 4.6 %collective-permute-done.7 = f32[320,128]{1,0:T(8,128)S(1)} collective-permute-done((f32[320,128]{1,0:T(8,128)S(1)}, f32[320,128]{1,0:T(8,128)S(1)}, u32[]{:S(2)}, u32[]{:S(2)}) %collective-permute-start.7) | collective-permute-done | bytes 163872 | tf_op jit(solution)/shard_map/ppermute | solution.py:380
  95.3 0.3 collective-permute-start.8
  95.6 5.1 %collective-permute-done.8 = f32[320,128]{1,0:T(8,128)S(1)} collective-permute-done((f32[320,128]{1,0:T(8,128)S(1)}, f32[320,128]{1,0:T(8,128)S(1)}, u32[]{:S(2)}, u32[]{:S(2)}) %collective-permute-start.8) | collective-permute-done | bytes 163872 | tf_op jit(solution)/shard_map/ppermute | solution.py:380
  100.8 0.5 collective-permute-start.9
  101.3 7.2 %collective-permute-done.9 = f32[320,128]{1,0:T(8,128)S(1)} collective-permute-done((f32[320,128]{1,0:T(8,128)S(1)}, f32[320,128]{1,0:T(8,128)S(1)}, u32[]{:S(2)}, u32[]{:S(2)}) %collective-permute-start.9) | collective-permute-done | bytes 163872 | tf_op jit(solution)/shard_map/ppermute | solution.py:380
  108.5 0.8 collective-permute-start.10
  109.2 4.6 %collective-permute-done.10 = f32[320,128]{1,0:T(8,128)S(1)} collective-permute-done((f32[320,128]{1,0:T(8,128)S(1)}, f32[320,128]{1,0:T(8,128)S(1)}, u32[]{:S(2)}, u32[]{:S(2)}) %collective-permute-start.10) | collective-permute-done | bytes 163872 | tf_op jit(solution)/shard_map/ppermute | solution.py:380
  114.0 0.9 copy.11.seed_ref
  114.9 0.7 collective-permute-done.11
  115.7 0.9 pad_maximum_fusion.corr_ref
  116.6 8.6 %first_weights.1 = (bf16[192,512]{1,0:T(8,128)(2,1)}, f32[512,512]{1,0:T(8,128)}) custom-call(f32[1280,128]{1,0:T(8,128)} %pad_maximum_fusion.corr_ref, s32[512,64]{1,0:T(8,128)} %copy.11.seed_ref), custom_call_target="tpu_custom_call" | custom-call | tf_op jit(solution)/shard_map/first_weights/pallas_call | solution.py:297
  125.2 0.9 copy-done.6
  126.1 12.6 %next_mixer.2 = f32[64,512]{1,0:T(8,128)S(1)} custom-call(bf16[192,512]{1,0:T(8,128)(2,1)S(1)} %copy-done.6, bf16[512,16384]{1,0:T(8,128)(2,1)} %get-tuple-element.9.fill_ref), custom_call_target="tpu_custom_call" | custom-call | tf_op jit(solution)/shard_map/next_mixer/pallas_call | solution.py:330
  138.9 1.1 collective-permute-done.12
  140.1 0.8 collective-permute-start.13
  140.8 3.6 %collective-permute-done.13 = f32[32,512]{1,0:T(8,128)S(1)} collective-permute-done((f32[32,512]{1,0:T(8,128)S(1)}, f32[32,512]{1,0:T(8,128)S(1)}, u32[]{:S(2)}, u32[]{:S(2)}) %collective-permute-start.13) | collective-permute-done | bytes 65568 | tf_op jit(solution)/shard_map/ppermute | solution.py:380
  144.4 0.8 collective-permute-start.14
  145.2 3.6 %collective-permute-done.14 = f32[32,512]{1,0:T(8,128)S(1)} collective-permute-done((f32[32,512]{1,0:T(8,128)S(1)}, f32[32,512]{1,0:T(8,128)S(1)}, u32[]{:S(2)}, u32[]{:S(2)}) %collective-permute-start.14) | collective-permute-done | bytes 65568 | tf_op jit(solution)/shard_map/ppermute | solution.py:380
  148.8 4.3 %collective-permute-done.15 = f32[32,512]{1,0:T(8,128)S(1)} collective-permute-done((f32[32,512]{1,0:T(8,128)S(1)}, f32[32,512]{1,0:T(8,128)S(1)}, u32[]{:S(2)}, u32[]{:S(2)}) %collective-permute-start.15) | collective-permute-done | bytes 65568 | tf_op jit(solution)/shard_map/ppermute | solution.py:380
  153.2 5.7 %collective-permute-done.16 = f32[32,512]{1,0:T(8,128)S(1)} collective-permute-done((f32[32,512]{1,0:T(8,128)S(1)}, f32[32,512]{1,0:T(8,128)S(1)}, u32[]{:S(2)}, u32[]{:S(2)}) %collective-permute-start.16) | collective-permute-done | bytes 65568 | tf_op jit(solution)/shard_map/ppermute | solution.py:380
  159.0 1.2 collective-permute-done.17
  160.3 0.7 pad_maximum_fusion.3.mixer_ref
  160.9 8.6 %later_weights.2.weights_ref = bf16[192,512]{1,0:T(8,128)(2,1)} custom-call(f32[512,512]{1,0:T(8,128)} %get-tuple-element.7.full_ref, f32[64,512]{1,0:T(8,128)} %pad_maximum_fusion.3.mixer_ref), custom_call_target="tpu_custom_call" | custom-call | tf_op jit(solution)/shard_map/later_weights/pallas_call | solution.py:308
  169.5 0.9 copy-done.4
  170.4 12.6 %next_mixer.3 = f32[64,512]{1,0:T(8,128)S(1)} custom-call(bf16[192,512]{1,0:T(8,128)(2,1)S(1)} %copy-done.4, bf16[512,16384]{1,0:T(8,128)(2,1)} %get-tuple-element.9.fill_ref), custom_call_target="tpu_custom_call" | custom-call | tf_op jit(solution)/shard_map/next_mixer/pallas_call | solution.py:330
  183.2 1.1 collective-permute-done.18
  184.4 0.8 collective-permute-start.19
  185.1 3.6 %collective-permute-done.19 = f32[32,512]{1,0:T(8,128)S(1)} collective-permute-done((f32[32,512]{1,0:T(8,128)S(1)}, f32[32,512]{1,0:T(8,128)S(1)}, u32[]{:S(2)}, u32[]{:S(2)}) %collective-permute-start.19) | collective-permute-done | bytes 65568 | tf_op jit(solution)/shard_map/ppermute | solution.py:380
  188.7 0.8 collective-permute-start.20
  189.5 3.6 %collective-permute-done.20 = f32[32,512]{1,0:T(8,128)S(1)} collective-permute-done((f32[32,512]{1,0:T(8,128)S(1)}, f32[32,512]{1,0:T(8,128)S(1)}, u32[]{:S(2)}, u32[]{:S(2)}) %collective-permute-start.20) | collective-permute-done | bytes 65568 | tf_op jit(solution)/shard_map/ppermute | solution.py:380
  193.1 4.3 %collective-permute-done.21 = f32[32,512]{1,0:T(8,128)S(1)} collective-permute-done((f32[32,512]{1,0:T(8,128)S(1)}, f32[32,512]{1,0:T(8,128)S(1)}, u32[]{:S(2)}, u32[]{:S(2)}) %collective-permute-start.21) | collective-permute-done | bytes 65568 | tf_op jit(solution)/shard_map/ppermute | solution.py:380
  197.5 5.7 %collective-permute-done.22 = f32[32,512]{1,0:T(8,128)S(1)} collective-permute-done((f32[32,512]{1,0:T(8,128)S(1)}, f32[32,512]{1,0:T(8,128)S(1)}, u32[]{:S(2)}, u32[]{:S(2)}) %collective-permute-start.22) | collective-permute-done | bytes 65568 | tf_op jit(solution)/shard_map/ppermute | solution.py:380
  203.3 0.7 copy.12
  204.0 0.5 collective-permute-done.23
  204.5 0.7 pad_maximum_fusion.4.mixer_ref
  205.2 5.7 %later_weights.3.weights_ref = bf16[96,512]{1,0:T(8,128)(2,1)} custom-call(f32[512,512]{1,0:T(8,128)} %get-tuple-element.7.full_ref, f32[64,512]{1,0:T(8,128)} %pad_maximum_fusion.4.mixer_ref), custom_call_target="tpu_custom_call" | custom-call | tf_op jit(solution)/shard_map/later_weights/pallas_call | solution.py:308
  210.9 0.9 copy-done.5
  211.8 10.4 %project_basis.1 = f32[32,16384]{1,0:T(8,128)} custom-call(bf16[96,512]{1,0:T(8,128)(2,1)S(1)} %copy-done.5, bf16[512,16384]{1,0:T(8,128)(2,1)} %get-tuple-element.9.fill_ref), custom_call_target="tpu_custom_call" | custom-call | tf_op jit(solution)/shard_map/project_basis/pallas_call | solution.py:353
  (59 shorter events, 1.9 us)
Async XLA Ops:
  0.6 1.2 copy-start
  1.9 0.9 copy-start.2
  16.8 2.2 %collective-permute-start = (f32[256,640]{1,0:T(8,128)S(1)}, f32[256,640]{1,0:T(8,128)S(1)}, u32[]{:S(2)}, u32[]{:S(2)}) collective-permute-start(f32[256,640]{1,0:T(8,128)S(1)} %constant_dynamic-slice_fusion.8), channel_id=1, source_target_pairs={{0,4},{4,0},{8,12},{12,8},{16,20},{20,16},{24,28},{28,24},{1,5},{5... | collective-permute-start | bytes 1966088 | tf_op jit(solution)/shard_map/ppermute | solution.py:380
  19.2 8.0 %collective-permute-start.1 = (f32[128,640]{1,0:T(8,128)S(1)}, f32[128,640]{1,0:T(8,128)S(1)}, u32[]{:S(2)}, u32[]{:S(2)}) collective-permute-start(f32[128,640]{1,0:T(8,128)S(1)} %constant_dynamic-slice_fusion.7), channel_id=1, source_target_pairs={{0,8},{4,20},{8,0},{12,28},{16,24},{20,4},{24,16},{28,12},{1,9},{5... | collective-permute-start | bytes 983048 | tf_op jit(solution)/shard_map/ppermute | solution.py:380
  27.2 5.4 %collective-permute-start.2 = (f32[64,640]{1,0:T(8,128)S(1)}, f32[64,640]{1,0:T(8,128)S(1)}, u32[]{:S(2)}, u32[]{:S(2)}) collective-permute-start(f32[64,640]{1,0:T(8,128)S(1)} %constant_dynamic-slice_fusion.6), channel_id=1, source_target_pairs={{0,16},{4,12},{8,24},{12,4},{16,0},{20,28},{24,8},{28,20},{1,17},{... | collective-permute-start | bytes 491528 | tf_op jit(solution)/shard_map/ppermute | solution.py:380
  29.4 33.4 %copy-start.1 = (bf16[32,16384]{1,0:T(8,128)(2,1)S(1)}, bf16[32,16384]{1,0:T(8,128)(2,1)}, u32[]{:S(2)}) copy-start(bf16[32,16384]{1,0:T(8,128)(2,1)} %basis_ref.3) | copy-start | bytes 3145732
  29.4 33.4 %copy-start.3 = (s32[512,128]{1,0:T(8,128)S(1)}, s32[512,128]{1,0:T(8,128)}, u32[]{:S(2)}) copy-start(s32[512,128]{1,0:T(8,128)} %flags_ref.3) | copy-start | bytes 786436
  32.7 4.6 %collective-permute-start.3 = (f32[32,640]{1,0:T(8,128)S(1)}, f32[32,640]{1,0:T(8,128)S(1)}, u32[]{:S(2)}, u32[]{:S(2)}) collective-permute-start(f32[32,640]{1,0:T(8,128)S(1)} %constant_dynamic-slice_fusion.5), channel_id=1, source_target_pairs={{0,1},{1,0},{2,3},{3,2},{4,5},{5,4},{6,7},{7,6},{8,9},{9,8},{10,11... | collective-permute-start | bytes 245768 | tf_op jit(solution)/shard_map/ppermute | solution.py:380
  37.3 5.3 %collective-permute-start.4 = (f32[16,640]{1,0:T(8,128)S(1)}, f32[16,640]{1,0:T(8,128)S(1)}, u32[]{:S(2)}, u32[]{:S(2)}) collective-permute-start(f32[16,640]{1,0:T(8,128)S(1)} %constant_dynamic-slice_fusion.4), channel_id=1, source_target_pairs={{0,2},{1,3},{2,0},{3,1},{4,6},{5,7},{6,4},{7,5},{8,10},{9,11},{10,... | collective-permute-start | bytes 122888 | tf_op jit(solution)/shard_map/ppermute | solution.py:380
  47.3 14.0 %all-to-all-start = ((f32[32,1,512]{2,1,0:T(1,128)}), f32[32,1,512]{2,1,0:T(1,128)S(1)}, u32[]{:S(2)}, u32[]{:S(2)}) async-start(f32[32,1,512]{2,1,0:T(1,128)} %reshape.13), calls=%async_computation | async-start | bytes 131072 | tf_op jit(solution)/shard_map/all_to_all | solution.py:418
  82.8 1.7 collective-permute-start.5
  82.9 31.2 %copy-start.7 = (s32[512,64]{0,1:T(8,128)S(1)}, s32[512,64]{0,1:T(8,128)}, u32[]{:S(2)}) copy-start(s32[512,64]{0,1:T(8,128)} %param.7) | copy-start | bytes 393220
  84.5 5.4 %collective-permute-start.6 = (f32[320,128]{1,0:T(8,128)S(1)}, f32[320,128]{1,0:T(8,128)S(1)}, u32[]{:S(2)}, u32[]{:S(2)}) collective-permute-start(f32[320,128]{1,0:T(8,128)S(1)} %constant_dynamic-slice_fusion.2), channel_id=1, source_target_pairs={{0,8},{4,20},{8,0},{12,28},{16,24},{20,4},{24,16},{28,12},{1,9},{5... | collective-permute-start | bytes 491528 | tf_op jit(solution)/shard_map/ppermute | solution.py:380
  89.9 5.4 %collective-permute-start.7 = (f32[320,128]{1,0:T(8,128)S(1)}, f32[320,128]{1,0:T(8,128)S(1)}, u32[]{:S(2)}, u32[]{:S(2)}) collective-permute-start(f32[320,128]{1,0:T(8,128)S(1)} %dynamic-slice_add_fusion.3), channel_id=1, source_target_pairs={{0,16},{4,12},{8,24},{12,4},{16,0},{20,28},{24,8},{28,20},{1,17},{... | collective-permute-start | bytes 491528 | tf_op jit(solution)/shard_map/ppermute | solution.py:380
  95.3 5.4 %collective-permute-start.8 = (f32[320,128]{1,0:T(8,128)S(1)}, f32[320,128]{1,0:T(8,128)S(1)}, u32[]{:S(2)}, u32[]{:S(2)}) collective-permute-start(f32[320,128]{1,0:T(8,128)S(1)} %add.131), channel_id=1, source_target_pairs={{0,1},{1,0},{2,3},{3,2},{4,5},{5,4},{6,7},{7,6},{8,9},{9,8},{10,11... | collective-permute-start | bytes 491528 | tf_op jit(solution)/shard_map/ppermute | solution.py:380
  100.8 7.7 %collective-permute-start.9 = (f32[320,128]{1,0:T(8,128)S(1)}, f32[320,128]{1,0:T(8,128)S(1)}, u32[]{:S(2)}, u32[]{:S(2)}) collective-permute-start(f32[320,128]{1,0:T(8,128)S(1)} %add.132), channel_id=1, source_target_pairs={{0,2},{1,3},{2,0},{3,1},{4,6},{5,7},{6,4},{7,5},{8,10},{9,11},{10,... | collective-permute-start | bytes 491528 | tf_op jit(solution)/shard_map/ppermute | solution.py:380
  108.5 5.4 %collective-permute-start.10 = (f32[320,128]{1,0:T(8,128)S(1)}, f32[320,128]{1,0:T(8,128)S(1)}, u32[]{:S(2)}, u32[]{:S(2)}) collective-permute-start(f32[320,128]{1,0:T(8,128)S(1)} %add.133), channel_id=1, source_target_pairs={{0,8},{4,20},{8,0},{12,28},{16,24},{20,4},{24,16},{28,12},{1,9},{5... | collective-permute-start | bytes 491528 | tf_op jit(solution)/shard_map/ppermute | solution.py:380
  113.9 1.7 collective-permute-start.11
  125.2 0.9 copy-start.6
  138.7 1.3 collective-permute-start.12
  140.1 4.3 %collective-permute-start.13 = (f32[32,512]{1,0:T(8,128)S(1)}, f32[32,512]{1,0:T(8,128)S(1)}, u32[]{:S(2)}, u32[]{:S(2)}) collective-permute-start(f32[32,512]{1,0:T(8,128)S(1)} %dynamic-slice_add_fusion.7), channel_id=1, source_target_pairs={{0,8},{4,20},{8,0},{12,28},{16,24},{20,4},{24,16},{28,12},{1,9},{5... | collective-permute-start | bytes 196616 | tf_op jit(solution)/shard_map/ppermute | solution.py:380
  144.4 4.3 %collective-permute-start.14 = (f32[32,512]{1,0:T(8,128)S(1)}, f32[32,512]{1,0:T(8,128)S(1)}, u32[]{:S(2)}, u32[]{:S(2)}) collective-permute-start(f32[32,512]{1,0:T(8,128)S(1)} %add.137), channel_id=1, source_target_pairs={{0,16},{4,12},{8,24},{12,4},{16,0},{20,28},{24,8},{28,20},{1,17},{... | collective-permute-start | bytes 196616 | tf_op jit(solution)/shard_map/ppermute | solution.py:380
  148.8 4.3 %collective-permute-start.15 = (f32[32,512]{1,0:T(8,128)S(1)}, f32[32,512]{1,0:T(8,128)S(1)}, u32[]{:S(2)}, u32[]{:S(2)}) collective-permute-start(f32[32,512]{1,0:T(8,128)S(1)} %add.138), channel_id=1, source_target_pairs={{0,1},{1,0},{2,3},{3,2},{4,5},{5,4},{6,7},{7,6},{8,9},{9,8},{10,11... | collective-permute-start | bytes 196616 | tf_op jit(solution)/shard_map/ppermute | solution.py:380
  153.1 5.8 %collective-permute-start.16 = (f32[32,512]{1,0:T(8,128)S(1)}, f32[32,512]{1,0:T(8,128)S(1)}, u32[]{:S(2)}, u32[]{:S(2)}) collective-permute-start(f32[32,512]{1,0:T(8,128)S(1)} %add.139), channel_id=1, source_target_pairs={{0,2},{1,3},{2,0},{3,1},{4,6},{5,7},{6,4},{7,5},{8,10},{9,11},{10,... | collective-permute-start | bytes 196616 | tf_op jit(solution)/shard_map/ppermute | solution.py:380
  158.9 1.3 collective-permute-start.17
  169.5 0.9 copy-start.4
  183.0 1.3 collective-permute-start.18
  184.4 4.3 %collective-permute-start.19 = (f32[32,512]{1,0:T(8,128)S(1)}, f32[32,512]{1,0:T(8,128)S(1)}, u32[]{:S(2)}, u32[]{:S(2)}) collective-permute-start(f32[32,512]{1,0:T(8,128)S(1)} %dynamic-slice_add_fusion.6), channel_id=1, source_target_pairs={{0,8},{4,20},{8,0},{12,28},{16,24},{20,4},{24,16},{28,12},{1,9},{5... | collective-permute-start | bytes 196616 | tf_op jit(solution)/shard_map/ppermute | solution.py:380
  188.7 4.3 %collective-permute-start.20 = (f32[32,512]{1,0:T(8,128)S(1)}, f32[32,512]{1,0:T(8,128)S(1)}, u32[]{:S(2)}, u32[]{:S(2)}) collective-permute-start(f32[32,512]{1,0:T(8,128)S(1)} %add.142), channel_id=1, source_target_pairs={{0,16},{4,12},{8,24},{12,4},{16,0},{20,28},{24,8},{28,20},{1,17},{... | collective-permute-start | bytes 196616 | tf_op jit(solution)/shard_map/ppermute | solution.py:380
  193.1 4.3 %collective-permute-start.21 = (f32[32,512]{1,0:T(8,128)S(1)}, f32[32,512]{1,0:T(8,128)S(1)}, u32[]{:S(2)}, u32[]{:S(2)}) collective-permute-start(f32[32,512]{1,0:T(8,128)S(1)} %add.143), channel_id=1, source_target_pairs={{0,1},{1,0},{2,3},{3,2},{4,5},{5,4},{6,7},{7,6},{8,9},{9,8},{10,11... | collective-permute-start | bytes 196616 | tf_op jit(solution)/shard_map/ppermute | solution.py:380
  197.4 5.8 %collective-permute-start.22 = (f32[32,512]{1,0:T(8,128)S(1)}, f32[32,512]{1,0:T(8,128)S(1)}, u32[]{:S(2)}, u32[]{:S(2)}) collective-permute-start(f32[32,512]{1,0:T(8,128)S(1)} %add.144), channel_id=1, source_target_pairs={{0,2},{1,3},{2,0},{3,1},{4,6},{5,7},{6,4},{7,5},{8,10},{9,11},{10,... | collective-permute-start | bytes 196616 | tf_op jit(solution)/shard_map/ppermute | solution.py:380
  203.2 1.3 collective-permute-start.23
  210.9 0.9 copy-start.5

commit v2 on v1

v2 whole, which is shorter than its diff:
```python
import functools
import math

import jax
import jax.numpy as jnp
from jax import lax
from jax.experimental import pallas as pl
from jax.experimental.pallas import tpu as pltpu
from jax.sharding import PartitionSpec as P

POWER = 2
DAMPING = 0.005
AXES = ("rows", "sub")
LANES = 128
SUBLANES = 8
SCRATCH_BYTES = 48 << 20
HIGHEST = lax.Precision.HIGHEST
F32 = jnp.float32
BF16 = jnp.bfloat16

CONTRACT_LANES = (((1,), (1,)), ((), ()))


def dot_nt(left, right, precision=None):
    return lax.dot_general(
        left, right, CONTRACT_LANES, precision=precision, preferred_element_type=F32
    )


def dot_nn(left, right, precision=None):
    return jnp.dot(left, right, precision=precision, preferred_element_type=F32)


def split_three(values):
    first = values.astype(BF16)
    rest = values - first.astype(F32)
    second = rest.astype(BF16)
    third = (rest - second.astype(F32)).astype(BF16)
    return first, second, third


def chunk_copy(source, target, arrived, step, chunk):
    part = chunk_at(step, chunk)
    return pltpu.make_async_copy(source.at[:, part], target.at[:, part], arrived.at[step])


def fetch_all(source, target, arrived, chunk):
    for step in range(target.shape[1] // chunk):
        chunk_copy(source, target, arrived, step, chunk).start()


def flag_columns(flags, step, blocks_step):
    shift = lax.rem(LANES - step * blocks_step, LANES)
    return pltpu.roll(flags, shift, 1).astype(BF16)


def chunk_at(step, chunk):
    return pl.ds(pl.multiple_of(step * chunk, chunk), chunk)


def normal_kernel(
    chunk,
    flags_ref,
    snap_hbm,
    basis_ref,
    out_ref,
    masked_hbm,
    snap_ref,
    masked_ref,
    gram_ref,
    right_ref,
    arrived,
    left,
):
    count, rows = snap_ref.shape
    modes = basis_ref.shape[0]
    half = modes // 2
    blocks_step = chunk // LANES
    steps = rows // chunk

    fetch_all(snap_hbm, snap_ref, arrived, chunk)
    right_ref[...] = jnp.zeros_like(right_ref)
    all_flags = flags_ref[...].astype(F32)

    for block in range(rows // LANES):
        piece = basis_ref[:, block * LANES : (block + 1) * LANES]
        copies = jnp.concatenate([piece] * (LANES // modes), axis=0)
        gram_ref[block * modes : (block + 1) * modes, :] = dot_nt(piece, copies)

    def body(step, carry):
        chunk_copy(snap_hbm, snap_ref, arrived, step, chunk).wait()
        columns = flag_columns(all_flags, step, blocks_step)
        here = chunk_at(step, chunk)
        source, target = snap_ref.at[:, here], masked_ref.at[:, here]
        for block in range(blocks_step):
            part = pl.ds(block * LANES, LANES)
            weight = jnp.broadcast_to(columns[:, block : block + 1], (count, LANES))
            target[:, part] = source[:, part] * weight
        chunk_copy(masked_ref, masked_hbm, left, step, chunk).start()
        right_ref[...] += dot_nt(target[...], basis_ref[:, here])
        return carry

    def drain(step, carry):
        chunk_copy(masked_ref, masked_hbm, left, step, chunk).wait()
        return carry

    lax.fori_loop(0, steps, body, 0)

    lane = lax.broadcasted_iota(jnp.int32, (LANES, LANES), 1)
    group = LANES // half
    tiles = []
    middle = jnp.zeros((LANES, LANES), F32)
    for tile_index in range(modes // group):
        tile = jnp.zeros((LANES, LANES), F32)
        for inner in range(group):
            mode = tile_index * group + inner
            entries = gram_ref[pl.ds(mode, LANES, stride=modes), :]
            moved = pltpu.roll(entries, (half * inner - mode) % LANES, 1)
            tile = jnp.where(lane // half == inner, moved, tile)
            if mode < half:
                middle = jnp.where(lane == mode + half, entries, middle)
        tiles.append(tile)
    tiles.append(middle)
    flags = flags_ref[...].astype(BF16)
    total = sum(
        dot_nn(flags, part) for part in split_three(jnp.concatenate(tiles, axis=1))
    )
    wide = LANES * (len(tiles) - 1)
    out_ref[:, :wide] = total[:, :wide]
    right = jnp.concatenate(
        [
            jnp.zeros((count, modes), F32),
            right_ref[...],
            jnp.zeros((count, LANES - 2 * modes), F32),
        ],
        axis=1,
    )
    out_ref[:, wide:] = total[:, wide:] + right
    lax.fori_loop(0, steps, drain, 0)


def normal_terms(flags, snapshots, basis, chunk=4096):
    count, rows = snapshots.shape
    modes = basis.shape[0]
    blocks = flags.shape[1]
    width = modes * modes // 2 + LANES
    whole = pl.BlockSpec(memory_space=pltpu.VMEM)
    return pl.pallas_call(
        functools.partial(normal_kernel, chunk),
        in_specs=[whole, pl.BlockSpec(memory_space=pl.ANY), whole],
        out_specs=[whole, pl.BlockSpec(memory_space=pl.ANY)],
        out_shape=[
            jax.ShapeDtypeStruct((count, width), F32),
            jax.ShapeDtypeStruct((count, rows), BF16),
        ],
        scratch_shapes=[
            pltpu.VMEM((count, rows), BF16),
            pltpu.VMEM((count, rows), BF16),
            pltpu.VMEM((blocks * modes, LANES), F32),
            pltpu.VMEM((count, modes), F32),
            pltpu.SemaphoreType.DMA((rows // chunk,)),
            pltpu.SemaphoreType.DMA((rows // chunk,)),
        ],
        compiler_params=pltpu.CompilerParams(vmem_limit_bytes=SCRATCH_BYTES),
        name="normal_terms",
    )(flags, snapshots, basis)


def solve_kernel(modes, shift, in_ref, out_ref, turned_ref, system_ref):
    half = modes // 2
    count, width = in_ref.shape
    padded = jnp.concatenate([in_ref[...], jnp.zeros((LANES - count, width), F32)], axis=0)
    turned_ref[...] = padded.T
    for mode in range(modes):
        first = min(half, modes - mode)
        base = mode * half
        start = mode * modes + mode
        values = turned_ref[base : base + first, :]
        system_ref[start : start + first, :] = values
        if first < half:
            wrapped = turned_ref[base + first : base + half, :]
            system_ref[pl.ds(mode, half - first, stride=modes), :] = wrapped
    middle = modes * half + half
    system_ref[pl.ds(half, half, stride=modes + 1), :] = turned_ref[middle : middle + half, :]
    right = turned_ref[modes * half + modes : modes * half + 2 * modes, :]
    index = lax.broadcasted_iota(jnp.int32, (modes, LANES), 0)

    rows = [system_ref[k * modes : (k + 1) * modes, :] for k in range(modes)]
    scaled = []
    targets = []
    for column in range(modes):
        row = jnp.where(index == column, rows[column] + shift, rows[column])
        inverse = 1.0 / row[column : column + 1, :]
        factor = jnp.where(index > column, row * inverse, 0.0)
        target = right[column : column + 1, :]
        scaled.append(factor)
        targets.append(target * inverse)
        right = right - factor * target
        for k in range(column + 1, modes):
            rows[k] = rows[k] - factor[k : k + 1, :] * row
    result = jnp.zeros((modes, LANES), F32)
    for column in reversed(range(modes)):
        value = targets[column] - jnp.sum(scaled[column] * result, axis=0, keepdims=True)
        result = jnp.where(index == column, value, result)
    square = jnp.concatenate([result, jnp.zeros((LANES - modes, LANES), F32)], axis=0)
    share = square.T[:count, :modes]
    high = out_ref.shape[1]
    dense = jnp.concatenate(
        [share[top : top + high, :] for top in range(0, count, high)], axis=1
    )
    for device in range(out_ref.shape[0]):
        out_ref[device] = dense


def solve_share(share, modes, rows_all, devices):
    count, width = share.shape
    return pl.pallas_call(
        functools.partial(solve_kernel, modes, DAMPING * rows_all),
        out_shape=jax.ShapeDtypeStruct((devices, count * modes // LANES, LANES), F32),
        scratch_shapes=[
            pltpu.VMEM((width, LANES), F32),
            pltpu.VMEM((modes * modes, LANES), F32),
        ],
        name="solve_share",
    )(share)


def packed_blocks(tiles):
    return [(i, (i + d) % tiles) for d in range(tiles // 2) for i in range(tiles)] + [
        (i, i + tiles // 2) for i in range(tiles // 2)
    ]


def refill_kernel(
    chunk,
    order,
    flags_ref,
    masked_hbm,
    basis_ref,
    shares_ref,
    fill_hbm,
    corr_ref,
    turned_ref,
    masked_ref,
    coef_ref,
    fill_ref,
    gap_ref,
    square_ref,
    sum_ref,
    arrived,
    left,
):
    count, rows = fill_ref.shape
    modes = basis_ref.shape[0]
    blocks = flags_ref.shape[1]
    group = square_ref.shape[1] // modes
    steps = rows // chunk
    side = count // 2
    fetch_all(masked_hbm, masked_ref, arrived, chunk)
    sum_ref[...] = jnp.zeros_like(sum_ref)
    square_ref[...] = jnp.zeros_like(square_ref)

    devices, high, _ = shares_ref.shape
    share_rows = count // devices
    for device in range(devices):
        dense = shares_ref[device]
        for place in range(share_rows // high):
            top = order[device] * share_rows + place * high
            coef_ref[top : top + high, :] = dense[:, place * modes : (place + 1) * modes]
    turned_ref[...] = coef_ref[...].T

    gaps = (1 - flags_ref[...]).astype(F32).astype(BF16)
    coef = coef_ref[...].astype(BF16).astype(F32)
    wide = jnp.concatenate([coef] * (2 * LANES // modes), axis=1)
    place = lax.broadcasted_iota(jnp.int32, (blocks, 2 * LANES), 0)
    owner = lax.broadcasted_iota(jnp.int32, (blocks, 2 * LANES), 1) // modes
    for part in range(blocks * modes // (2 * LANES)):
        first = part * (2 * LANES // modes)
        pick = jnp.where(place == owner + first, 1.0, 0.0).astype(BF16)
        gap_ref[:, part * 2 * LANES : (part + 1) * 2 * LANES] = (
            dot_nn(gaps, pick) * wide
        ).astype(BF16)

    def body(step, carry):
        here = chunk_at(step, chunk)
        chunk_copy(masked_hbm, masked_ref, arrived, step, chunk).wait()
        basis = basis_ref.at[:, here]
        masked, filled = masked_ref.at[:, here], fill_ref.at[:, here]
        weights = gap_ref.at[:, chunk_at(step, chunk // LANES * modes)]
        span = group * LANES
        for part in range(chunk // span):
            square = square_ref.at[part]
            for inner in range(group):
                square[
                    inner * modes : (inner + 1) * modes, inner * LANES : (inner + 1) * LANES
                ] = basis[:, part * span + inner * LANES : part * span + (inner + 1) * LANES]
            own = weights[:, part * group * modes : (part + 1) * group * modes]
            recon = dot_nn(own, square[...]).astype(BF16)
            lanes = pl.ds(part * span, span)
            filled[:, lanes] = masked[:, lanes] + recon
        chunk_copy(fill_ref, fill_hbm, left, step, chunk).start()
        upper, lower = filled[:side, :], filled[side:, :]
        sum_ref[:side, :side] += dot_nt(upper, upper)
        sum_ref[:side, side:] += dot_nt(upper, lower)
        sum_ref[side:, side:] += dot_nt(lower, lower)
        return carry

    def drain(step, carry):
        chunk_copy(fill_ref, fill_hbm, left, step, chunk).wait()
        return carry

    lax.fori_loop(0, steps, body, 0)
    for place, (i, j) in enumerate(packed_blocks(count // LANES)):
        i, j = min(i, j), max(i, j)
        corr_ref[place * LANES : (place + 1) * LANES, :] = sum_ref[
            i * LANES : (i + 1) * LANES, j * LANES : (j + 1) * LANES
        ]
    lax.fori_loop(0, steps, drain, 0)


def refill_correlate(flags, masked, basis, shares, order, chunk=4096, group=8):
    count, rows = masked.shape
    modes = basis.shape[0]
    packed = len(packed_blocks(count // LANES)) * LANES
    whole = pl.BlockSpec(memory_space=pltpu.VMEM)
    hbm = pl.BlockSpec(memory_space=pl.ANY)
    return pl.pallas_call(
        functools.partial(refill_kernel, chunk, order),
        in_specs=[whole, hbm, whole, whole],
        out_specs=[hbm, whole, whole],
        out_shape=[
            jax.ShapeDtypeStruct((count, rows), BF16),
            jax.ShapeDtypeStruct((packed, LANES), F32),
            jax.ShapeDtypeStruct((modes, count), F32),
        ],
        scratch_shapes=[
            pltpu.VMEM((count, rows), BF16),
            pltpu.VMEM((count, modes), F32),
            pltpu.VMEM((count, rows), BF16),
            pltpu.VMEM((count, flags.shape[1] * modes), BF16),
            pltpu.VMEM((chunk // (group * LANES), group * modes, group * LANES), BF16),
            pltpu.VMEM((count, count), F32),
            pltpu.SemaphoreType.DMA((rows // chunk,)),
            pltpu.SemaphoreType.DMA((rows // chunk,)),
        ],
        compiler_params=pltpu.CompilerParams(vmem_limit_bytes=SCRATCH_BYTES),
        name="refill_correlate",
    )(flags, masked, basis, shares)


def inverse_cholesky(products, panel=4):
    extent = products.shape[0]
    shape = (SUBLANES, 2 * extent)
    sub = lax.broadcasted_iota(jnp.int32, shape, 0)
    lane = lax.broadcasted_iota(jnp.int32, shape, 1)
    tiles = []
    for top in range(0, extent, SUBLANES):
        left = products[top : top + SUBLANES, :]
        both = jnp.concatenate([left, jnp.zeros_like(left)], axis=1)
        tiles.append(jnp.where(lane == sub + top + extent, 1.0, both))
    pivots = [jnp.ones(shape, F32) for _ in tiles]
    for start in range(0, extent, panel):
        first = start // SUBLANES
        inside = range(start, start + panel)
        spread = {
            (column, t): jnp.broadcast_to(tiles[t][:, column : column + 1], shape)
            for column in inside
            for t in range(first, len(tiles))
        }
        for column in inside:
            home, place = divmod(column, SUBLANES)
            pivot = spread[column, home][place : place + 1, :]
            inverse = 1.0 / pivot
            pivots[home] = jnp.where(sub == place, pivot, pivots[home])
            row = tiles[home][place : place + 1, :] * inverse
            later = range(column + 1, start + panel)
            values = {c: spread[c, home][place : place + 1, :] * inverse for c in later}
            for t in range(home, len(tiles)):
                factor = spread[column, t]
                if t == home:
                    factor = jnp.where(sub > place, factor, 0.0)
                for c in later:
                    spread[c, t] = spread[c, t] - factor * values[c]
                tiles[t] = tiles[t] - factor * row
    scaled = [tile / jnp.sqrt(pivot) for tile, pivot in zip(tiles, pivots)]
    return jnp.concatenate(scaled, axis=0)[:, extent:]


def sweep_weights(mixer, full, rows):
    spread = dot_nn(mixer, full, HIGHEST)
    products = dot_nt(spread, mixer, HIGHEST)
    return dot_nn(inverse_cholesky(products)[:rows], mixer, HIGHEST)


def first_kernel(bit_ref, mine_ref, other_ref, seed_ref, out_ref, full_ref):
    count = full_ref.shape[0]
    corr = joined(bit_ref, mine_ref, other_ref)
    for place, (i, j) in enumerate(packed_blocks(count // LANES)):
        i, j = min(i, j), max(i, j)
        tile = corr[place * LANES : (place + 1) * LANES, :]
        rows, cols = pl.ds(i * LANES, LANES), pl.ds(j * LANES, LANES)
        full_ref[rows, cols] = tile
        if i != j:
            full_ref[cols, rows] = tile.T
    mixer = seed_ref[...].astype(F32).T
    store_parts(out_ref, sweep_weights(mixer, full_ref[...], mixer.shape[0]))


def later_kernel(rows, scale, bit_ref, mine_ref, other_ref, full_ref, out_ref):
    mixer = joined(bit_ref, mine_ref, other_ref).astype(BF16).astype(F32)
    store_parts(out_ref, sweep_weights(mixer, full_ref[...], rows) * scale)


def store_parts(out_ref, values):
    rows = values.shape[0]
    for place, part in enumerate(split_three(values)):
        out_ref[place * rows : (place + 1) * rows, :] = part


def joined(bit_ref, mine_ref, other_ref):
    low = bit_ref[0] == 0
    mine, other = mine_ref[...], other_ref[...]
    return jnp.concatenate(
        [jnp.where(low, mine, other), jnp.where(low, other, mine)], axis=0
    )


def weight_specs(halves):
    scalar = pl.BlockSpec(memory_space=pltpu.SMEM)
    return [scalar] + [pl.BlockSpec(memory_space=pltpu.VMEM)] * halves


def first_weights(halves, seed):
    count, width = seed.shape
    return pl.pallas_call(
        first_kernel,
        in_specs=weight_specs(3),
        out_shape=[
            pltpu.VMEM((3 * width, count), BF16),
            pltpu.VMEM((count, count), F32),
        ],
        name="first_weights",
    )(*halves, seed)


def later_weights(halves, full, rows, scale):
    return pl.pallas_call(
        functools.partial(later_kernel, rows, scale),
        in_specs=weight_specs(3),
        out_shape=pltpu.VMEM((3 * rows, full.shape[0]), BF16),
        name="later_weights",
    )(*halves, full)


def mixer_kernel(chunk, weights_ref, fill_hbm, out_ref, fill_ref, sum_ref, arrived):
    width = out_ref.shape[0]
    fetch_all(fill_hbm, fill_ref, arrived, chunk)
    sum_ref[...] = jnp.zeros_like(sum_ref)

    def body(step, carry):
        chunk_copy(fill_hbm, fill_ref, arrived, step, chunk).wait()
        filled = fill_ref[:, chunk_at(step, chunk)]
        terms = dot_nn(weights_ref[...], filled)
        ortho = terms[:width] + (terms[width : 2 * width] + terms[2 * width :])
        sum_ref[...] += dot_nt(filled, ortho.astype(BF16))
        return carry

    lax.fori_loop(0, fill_ref.shape[1] // chunk, body, 0)
    out_ref[...] = sum_ref[...].T


def next_mixer(weights, filled, chunk=4096):
    count, rows = filled.shape
    width = weights.shape[0] // 3
    whole = pl.BlockSpec(memory_space=pltpu.VMEM)
    return pl.pallas_call(
        functools.partial(mixer_kernel, chunk),
        in_specs=[whole, pl.BlockSpec(memory_space=pl.ANY)],
        out_specs=whole,
        out_shape=jax.ShapeDtypeStruct((width, count), F32),
        scratch_shapes=[
            pltpu.VMEM((count, rows), BF16),
            pltpu.VMEM((count, width), F32),
            pltpu.SemaphoreType.DMA((rows // chunk,)),
        ],
        compiler_params=pltpu.CompilerParams(vmem_limit_bytes=SCRATCH_BYTES),
        name="next_mixer",
    )(weights, filled)


def basis_kernel(chunk, weights_ref, fill_hbm, out_hbm, fill_ref, out_ref, arrived, left):
    modes, rows = out_ref.shape
    fetch_all(fill_hbm, fill_ref, arrived, chunk)

    def body(step, carry):
        here = chunk_at(step, chunk)
        chunk_copy(fill_hbm, fill_ref, arrived, step, chunk).wait()
        terms = dot_nn(weights_ref[...], fill_ref[:, here])
        out_ref[:, here] = terms[:modes] + (terms[modes : 2 * modes] + terms[2 * modes :])
        chunk_copy(out_ref, out_hbm, left, step, chunk).start()
        return carry

    def drain(step, carry):
        chunk_copy(out_ref, out_hbm, left, step, chunk).wait()
        return carry

    lax.fori_loop(0, rows // chunk, body, 0)
    lax.fori_loop(0, rows // chunk, drain, 0)


def project_basis(weights, filled, chunk=4096):
    count, rows = filled.shape
    modes = weights.shape[0] // 3
    hbm = pl.BlockSpec(memory_space=pl.ANY)
    return pl.pallas_call(
        functools.partial(basis_kernel, chunk),
        in_specs=[pl.BlockSpec(memory_space=pltpu.VMEM), hbm],
        out_specs=hbm,
        out_shape=jax.ShapeDtypeStruct((modes, rows), F32),
        scratch_shapes=[
            pltpu.VMEM((count, rows), BF16),
            pltpu.VMEM((modes, rows), F32),
            pltpu.SemaphoreType.DMA((rows // chunk,)),
            pltpu.SemaphoreType.DMA((rows // chunk,)),
        ],
        compiler_params=pltpu.CompilerParams(vmem_limit_bytes=SCRATCH_BYTES),
        name="project_basis",
    )(weights, filled)


class Stage:
    def __init__(self, axis, size, bits):
        self.axis = axis
        self.pairs = [(i, i ^ (1 << bits[i & 1])) for i in range(size)]
        self.bits = bits

    def bit(self):
        place = lax.axis_index(self.axis)
        if self.bits[0] == self.bits[1]:
            return (place >> self.bits[0]) & 1
        return jnp.where(place & 1, place >> self.bits[1], place >> self.bits[0]) & 1

    def swap(self, values):
        return lax.ppermute(values, self.axis, self.pairs)


def stages():
    rows, sub = (lax.axis_size(name) for name in AXES)
    high = list(range(1, rows.bit_length() - 1))
    plan = [Stage("rows", rows, (0, 0))]
    plan += [Stage("rows", rows, bits) for bits in zip(high, reversed(high))]
    plan += [Stage("sub", sub, (bit, bit)) for bit in range(sub.bit_length() - 1)]
    return plan


def halve(values, stage):
    bit = stage.bit()
    half = values.shape[0] // 2
    keep = lax.dynamic_slice_in_dim(values, bit * half, half, 0)
    send = lax.dynamic_slice_in_dim(values, (1 - bit) * half, half, 0)
    return keep + stage.swap(send)


def join(values, stage):
    other = stage.swap(values)
    low = stage.bit() == 0
    return jnp.concatenate(
        [jnp.where(low, values, other), jnp.where(low, other, values)], axis=0
    )


def scatter_sum(values):
    for stage in stages():
        values = halve(values, stage)
    return values


def share_order():
    rows, sub = (lax.axis_size(name) for name in AXES)
    order = []
    for row in range(rows):
        for column in range(sub):
            place = 0
            for stage in stages():
                index = row if stage.axis == "rows" else column
                place = 2 * place + ((index >> stage.bits[row & 1]) & 1)
            order.append(place)
    return order


def sum_everywhere(values, halvings):
    plan = stages()
    for stage in plan[:halvings]:
        values = halve(values, stage)
    for stage in plan[halvings:]:
        values = values + stage.swap(values)
    for stage in reversed(plan[1:halvings]):
        values = join(values, stage)
    core = plan[0]
    return core.bit().astype(jnp.int32).reshape(1), values, core.swap(values)


def per_device(old_basis, snapshots, gap_flags, sketch_seed):
    modes = old_basis.shape[0]
    rows_all = old_basis.shape[1] * lax.axis_size(AXES)
    terms, masked = normal_terms(gap_flags, snapshots, old_basis)
    devices = lax.axis_size(AXES)
    shares = solve_share(scatter_sum(terms), modes, rows_all, devices)
    shares = lax.all_to_all(shares, AXES, 0, 0, tiled=True)
    filled, corr, coefs = refill_correlate(gap_flags, masked, old_basis, shares, share_order())
    weights, full = first_weights(sum_everywhere(corr, 2), sketch_seed)
    width = sketch_seed.shape[1]
    for sweep in range(1, POWER + 1):
        halves = sum_everywhere(next_mixer(weights, filled), 1)
        if sweep < POWER:
            weights = later_weights(halves, full, width, 1.0)
        else:
            weights = later_weights(halves, full, modes, math.sqrt(rows_all))
    return project_basis(weights, filled), coefs


def solution(mesh):
    split = P(None, AXES)
    return jax.shard_map(
        per_device,
        mesh=mesh,
        in_specs=(split, split, split, P()),
        out_specs=(split, P()),
        check_vma=False,
    )
```

time: 223 us -> 196 us (0.88)
  Pallas kernels: 94.9 us -> 74 us
  local copies, waits for them, and re-layouts: 8.91 us -> 5.23 us
  other arithmetic: 4.14 us -> 1.02 us
    pallas_call x8, Pallas kernels: 92.4 us -> 71.3 us  [the longest x2 21.8 us: next_mixer(): pl.pallas_call(functools.partial(mixer_kernel, chunk), in_specs=[whole, p...]
    unnamed x21 -> x25, local copies, waits for them, and re-layouts: 7.44 us -> 5 us
  transfers between devices with their start and end apart: 25 -> 25, of which waited for: 25 -> 25; matrix products, arithmetic and copies ran while one was open for 1% -> 0% of each run, Pallas kernels for 0% -> 0%
where the time goes in v2:
time: 196 us; the launch traced here: 195 us
  waiting for transfers between devices  89.3 us (46%)
  Pallas kernels  74 us (38%)
  starting transfers between devices  24.6 us (13%)
  local copies, waits for them, and re-layouts  5.23 us (3%)
    ppermute x24, waiting for transfers between devices, swap(): return lax.ppermute(values, self.axis, self.pairs)  82 us
    pallas_call x2, Pallas kernels, next_mixer(): pl.pallas_call(functools.partial(mixer_kernel, chunk), in_specs=[whole, p...  21.8 us
    ppermute x24, starting transfers between devices, swap(): return lax.ppermute(values, self.axis, self.pairs)  18 us
    pallas_call x1, Pallas kernels, refill_correlate(): pl.pallas_call(functools.partial(refill_kernel, chunk, order), in_specs=[...  16.6 us
    pallas_call x1, Pallas kernels, normal_terms(): pl.pallas_call(functools.partial(normal_kernel, chunk), in_specs=[whole,...  12.1 us
    pallas_call x2, Pallas kernels, later_weights(): pl.pallas_call(functools.partial(later_kernel, rows, scale), in_specs=wei...  8.21 us
    pallas_call x1, Pallas kernels, project_basis(): pl.pallas_call(functools.partial(basis_kernel, chunk), in_specs=[pl.Block...  7.9 us
    all_to_all x1, waiting for transfers between devices, per_device(): shares = lax.all_to_all(shares, AXES, 0, 0, tiled=True)  7.32 us
  transfers between devices with their start and end apart: 25, of which 25 were waited for; matrix products, arithmetic and copies ran while one was open for 0% of the time, Pallas kernels for 0%

profile of v2, /device:TPU:0, one launch (start us, length us, event | category | flops | bytes accessed | tf_op | source)
XLA Modules:
  0.0 195.4 jit_solution(9683322794652290244)
XLA Ops:
  0.6 1.2 copy-done
  1.9 0.9 copy-done.3
  2.8 12.1 %normal_terms.1 = (f32[512,640]{1,0:T(8,128)S(1)}, bf16[512,16384]{1,0:T(8,128)(2,1)}) custom-call(s32[512,128]{1,0:T(8,128)S(1)} %copy-done.3, bf16[512,16384]{1,0:T(8,128)(2,1)} %snap_hbm.1, bf16[32,16384]{1,0:T(8,128)(2,1)S(1)} %copy-done), custom_call_target="tpu_custom_call" | custom-call | tf_op jit(solution)/shard_map/normal_terms/pallas_call | solution.py:148
  15.0 0.5 collective-permute-start
  15.5 1.7 collective-permute-done
  17.4 2.9 %collective-permute-start.1 = (f32[128,640]{1,0:T(8,128)S(1)}, f32[128,640]{1,0:T(8,128)S(1)}, u32[]{:S(2)}, u32[]{:S(2)}) collective-permute-start(f32[128,640]{1,0:T(8,128)S(1)} %constant_dynamic-slice_fusion.7), channel_id=1, source_target_pairs={{0,8},{4,20},{8,0},{12,28},{16,24},{20,4},{24,16},{28,12},{1,9},{5... | collective-permute-start | bytes 983048 | tf_op jit(solution)/shard_map/ppermute | solution.py:544
  20.3 5.1 %collective-permute-done.1 = f32[128,640]{1,0:T(8,128)S(1)} collective-permute-done((f32[128,640]{1,0:T(8,128)S(1)}, f32[128,640]{1,0:T(8,128)S(1)}, u32[]{:S(2)}, u32[]{:S(2)}) %collective-permute-start.1) | collective-permute-done | bytes 327712 | tf_op jit(solution)/shard_map/ppermute | solution.py:544
  25.4 2.1 %collective-permute-start.2 = (f32[64,640]{1,0:T(8,128)S(1)}, f32[64,640]{1,0:T(8,128)S(1)}, u32[]{:S(2)}, u32[]{:S(2)}) collective-permute-start(f32[64,640]{1,0:T(8,128)S(1)} %constant_dynamic-slice_fusion.6), channel_id=1, source_target_pairs={{0,16},{4,12},{8,24},{12,4},{16,0},{20,28},{24,8},{28,20},{1,17},{... | collective-permute-start | bytes 491528 | tf_op jit(solution)/shard_map/ppermute | solution.py:544
  27.5 3.3 %collective-permute-done.2 = f32[64,640]{1,0:T(8,128)S(1)} collective-permute-done((f32[64,640]{1,0:T(8,128)S(1)}, f32[64,640]{1,0:T(8,128)S(1)}, u32[]{:S(2)}, u32[]{:S(2)}) %collective-permute-start.2) | collective-permute-done | bytes 163872 | tf_op jit(solution)/shard_map/ppermute | solution.py:544
  30.9 2.1 %collective-permute-start.3 = (f32[32,640]{1,0:T(8,128)S(1)}, f32[32,640]{1,0:T(8,128)S(1)}, u32[]{:S(2)}, u32[]{:S(2)}) collective-permute-start(f32[32,640]{1,0:T(8,128)S(1)} %constant_dynamic-slice_fusion.5), channel_id=1, source_target_pairs={{0,1},{1,0},{2,3},{3,2},{4,5},{5,4},{6,7},{7,6},{8,9},{9,8},{10,11... | collective-permute-start | bytes 245768 | tf_op jit(solution)/shard_map/ppermute | solution.py:544
  33.0 2.4 %collective-permute-done.3 = f32[32,640]{1,0:T(8,128)S(1)} collective-permute-done((f32[32,640]{1,0:T(8,128)S(1)}, f32[32,640]{1,0:T(8,128)S(1)}, u32[]{:S(2)}, u32[]{:S(2)}) %collective-permute-start.3) | collective-permute-done | bytes 81952 | tf_op jit(solution)/shard_map/ppermute | solution.py:544
  35.5 3.3 %collective-permute-start.4 = (f32[16,640]{1,0:T(8,128)S(1)}, f32[16,640]{1,0:T(8,128)S(1)}, u32[]{:S(2)}, u32[]{:S(2)}) collective-permute-start(f32[16,640]{1,0:T(8,128)S(1)} %constant_dynamic-slice_fusion.4), channel_id=1, source_target_pairs={{0,2},{1,3},{2,0},{3,1},{4,6},{5,7},{6,4},{7,5},{8,10},{9,11},{10,... | collective-permute-start | bytes 122888 | tf_op jit(solution)/shard_map/ppermute | solution.py:544
  38.8 2.0 %collective-permute-done.4 = f32[16,640]{1,0:T(8,128)S(1)} collective-permute-done((f32[16,640]{1,0:T(8,128)S(1)}, f32[16,640]{1,0:T(8,128)S(1)}, u32[]{:S(2)}, u32[]{:S(2)}) %collective-permute-start.4) | collective-permute-done | bytes 40992 | tf_op jit(solution)/shard_map/ppermute | solution.py:544
  40.7 0.6 dynamic-slice_add_fusion.8.in_ref
  41.4 2.7 %solve_share.1 = f32[32,4,128]{2,1,0:T(4,128)} custom-call(f32[16,640]{1,0:T(8,128)} %dynamic-slice_add_fusion.8.in_ref), custom_call_target="tpu_custom_call" | custom-call | tf_op jit(solution)/shard_map/solve_share/pallas_call | solution.py:217
  44.0 6.6 %all-to-all-start = ((f32[32,4,128]{2,1,0:T(4,128)}), f32[32,4,128]{2,1,0:T(4,128)S(1)}, u32[]{:S(2)}, u32[]{:S(2)}) async-start(f32[32,4,128]{2,1,0:T(4,128)} %solve_share.1), calls=%async_computation | async-start | bytes 131072 | tf_op jit(solution)/shard_map/all_to_all | solution.py:609
  50.7 7.3 %all-to-all-done.shares_ref = f32[32,4,128]{2,1,0:T(4,128)S(1)} async-done(((f32[32,4,128]{2,1,0:T(4,128)}), f32[32,4,128]{2,1,0:T(4,128)S(1)}, u32[]{:S(2)}, u32[]{:S(2)}) %all-to-all-start) | async-done | bytes 65568 | tf_op jit(solution)/shard_map/all_to_all | solution.py:609
  58.0 16.6 %refill_correlate.1 = (bf16[512,16384]{1,0:T(8,128)(2,1)}, f32[1280,128]{1,0:T(8,128)S(1)}, f32[32,512]{1,0:T(8,128)}) custom-call(s32[512,128]{1,0:T(8,128)S(1)} %copy-done.4, bf16[512,16384]{1,0:T(8,128)(2,1)} %get-tuple-element.9.masked_hbm, bf16[32,16384]{1,0:T(8,128)(2,1)S(1)} %copy-done.1, f32[32,4,128]{2,1,0:T(4,128)S(1)} %all-to-all-done.shares_ref), custom_call_target="tpu_custom_call" | custom-call | tf_op jit(solution)/shard_map/refill_correlate/pallas_call | solution.py:327
  74.6 0.1 collective-permute-start.5
  74.7 1.6 collective-permute-done.5
  76.4 0.7 collective-permute-start.6
  77.1 4.7 %collective-permute-done.6 = f32[320,128]{1,0:T(8,128)S(1)} collective-permute-done((f32[320,128]{1,0:T(8,128)S(1)}, f32[320,128]{1,0:T(8,128)S(1)}, u32[]{:S(2)}, u32[]{:S(2)}) %collective-permute-start.6) | collective-permute-done | bytes 163872 | tf_op jit(solution)/shard_map/ppermute | solution.py:544
  81.8 0.7 collective-permute-start.7
  82.5 4.6 %collective-permute-done.7 = f32[320,128]{1,0:T(8,128)S(1)} collective-permute-done((f32[320,128]{1,0:T(8,128)S(1)}, f32[320,128]{1,0:T(8,128)S(1)}, u32[]{:S(2)}, u32[]{:S(2)}) %collective-permute-start.7) | collective-permute-done | bytes 163872 | tf_op jit(solution)/shard_map/ppermute | solution.py:544
  87.2 0.3 collective-permute-start.8
  87.5 5.1 %collective-permute-done.8 = f32[320,128]{1,0:T(8,128)S(1)} collective-permute-done((f32[320,128]{1,0:T(8,128)S(1)}, f32[320,128]{1,0:T(8,128)S(1)}, u32[]{:S(2)}, u32[]{:S(2)}) %collective-permute-start.8) | collective-permute-done | bytes 163872 | tf_op jit(solution)/shard_map/ppermute | solution.py:544
  92.6 0.5 collective-permute-start.9
  93.1 7.2 %collective-permute-done.9 = f32[320,128]{1,0:T(8,128)S(1)} collective-permute-done((f32[320,128]{1,0:T(8,128)S(1)}, f32[320,128]{1,0:T(8,128)S(1)}, u32[]{:S(2)}, u32[]{:S(2)}) %collective-permute-start.9) | collective-permute-done | bytes 163872 | tf_op jit(solution)/shard_map/ppermute | solution.py:544
  100.3 0.7 collective-permute-start.10
  101.1 4.6 %collective-permute-done.10 = f32[320,128]{1,0:T(8,128)S(1)} collective-permute-done((f32[320,128]{1,0:T(8,128)S(1)}, f32[320,128]{1,0:T(8,128)S(1)}, u32[]{:S(2)}, u32[]{:S(2)}) %collective-permute-start.10) | collective-permute-done | bytes 163872 | tf_op jit(solution)/shard_map/ppermute | solution.py:544
  105.8 0.1 collective-permute-start.11
  105.9 0.8 copy.6.seed_ref
  106.7 0.8 collective-permute-done.11.other_ref
  107.5 0.7 copy-done.6
  108.2 4.7 %first_weights.1 = (bf16[192,512]{1,0:T(8,128)(2,1)S(1)}, f32[512,512]{1,0:T(8,128)S(1)}) custom-call(s32[1]{0:T(128)} %bitcast.bit_ref, f32[640,128]{1,0:T(8,128)} %copy-done.5, f32[640,128]{1,0:T(8,128)} %copy-done.6, s32[512,64]{1,0:T(8,128)} %copy.6.seed_ref), custom_call_target="tpu_custom_call" | custom-call | tf_op jit(solution)/shard_map/first_weights/pallas_call | solution.py:435
  112.9 11.1 %next_mixer.2 = f32[64,512]{1,0:T(8,128)S(1)} custom-call(bf16[192,512]{1,0:T(8,128)(2,1)S(1)} %get-tuple-element.12.weights_ref, bf16[512,16384]{1,0:T(8,128)(2,1)} %get-tuple-element.13.fill_hbm), custom_call_target="tpu_custom_call" | custom-call | tf_op jit(solution)/shard_map/next_mixer/pallas_call | solution.py:476
  124.1 0.2 collective-permute-start.12
  124.3 1.1 collective-permute-done.12
  125.4 0.7 collective-permute-start.13
  126.1 3.6 %collective-permute-done.13 = f32[32,512]{1,0:T(8,128)S(1)} collective-permute-done((f32[32,512]{1,0:T(8,128)S(1)}, f32[32,512]{1,0:T(8,128)S(1)}, u32[]{:S(2)}, u32[]{:S(2)}) %collective-permute-start.13) | collective-permute-done | bytes 65568 | tf_op jit(solution)/shard_map/ppermute | solution.py:544
  129.7 0.8 collective-permute-start.14
  130.5 3.6 %collective-permute-done.14 = f32[32,512]{1,0:T(8,128)S(1)} collective-permute-done((f32[32,512]{1,0:T(8,128)S(1)}, f32[32,512]{1,0:T(8,128)S(1)}, u32[]{:S(2)}, u32[]{:S(2)}) %collective-permute-start.14) | collective-permute-done | bytes 65568 | tf_op jit(solution)/shard_map/ppermute | solution.py:544
  134.1 0.1 collective-permute-start.15
  134.2 4.3 %collective-permute-done.15 = f32[32,512]{1,0:T(8,128)S(1)} collective-permute-done((f32[32,512]{1,0:T(8,128)S(1)}, f32[32,512]{1,0:T(8,128)S(1)}, u32[]{:S(2)}, u32[]{:S(2)}) %collective-permute-start.15) | collective-permute-done | bytes 65568 | tf_op jit(solution)/shard_map/ppermute | solution.py:544
  138.5 5.7 %collective-permute-done.16 = f32[32,512]{1,0:T(8,128)S(1)} collective-permute-done((f32[32,512]{1,0:T(8,128)S(1)}, f32[32,512]{1,0:T(8,128)S(1)}, u32[]{:S(2)}, u32[]{:S(2)}) %collective-permute-start.16) | collective-permute-done | bytes 65568 | tf_op jit(solution)/shard_map/ppermute | solution.py:544
  144.3 0.1 collective-permute-start.17
  144.3 1.2 collective-permute-done.17.other_ref
  145.6 0.6 copy-done.11
  146.2 4.8 %later_weights.2.weights_ref = bf16[192,512]{1,0:T(8,128)(2,1)S(1)} custom-call(s32[1]{0:T(128)} %bitcast.bit_ref, f32[32,512]{1,0:T(8,128)} %copy-done.8, f32[32,512]{1,0:T(8,128)} %copy-done.11, f32[512,512]{1,0:T(8,128)} %copy-done.2), custom_call_target="tpu_custom_call" | custom-call | tf_op jit(solution)/shard_map/later_weights/pallas_call | solution.py:447
  150.9 10.7 %next_mixer.3 = f32[64,512]{1,0:T(8,128)S(1)} custom-call(bf16[192,512]{1,0:T(8,128)(2,1)S(1)} %later_weights.2.weights_ref, bf16[512,16384]{1,0:T(8,128)(2,1)} %get-tuple-element.13.fill_hbm), custom_call_target="tpu_custom_call" | custom-call | tf_op jit(solution)/shard_map/next_mixer/pallas_call | solution.py:476
  161.7 0.2 collective-permute-start.18
  161.9 1.1 collective-permute-done.18
  163.0 0.7 collective-permute-start.19
  163.8 3.6 %collective-permute-done.19 = f32[32,512]{1,0:T(8,128)S(1)} collective-permute-done((f32[32,512]{1,0:T(8,128)S(1)}, f32[32,512]{1,0:T(8,128)S(1)}, u32[]{:S(2)}, u32[]{:S(2)}) %collective-permute-start.19) | collective-permute-done | bytes 65568 | tf_op jit(solution)/shard_map/ppermute | solution.py:544
  167.4 0.8 collective-permute-start.20
  168.1 3.6 %collective-permute-done.20 = f32[32,512]{1,0:T(8,128)S(1)} collective-permute-done((f32[32,512]{1,0:T(8,128)S(1)}, f32[32,512]{1,0:T(8,128)S(1)}, u32[]{:S(2)}, u32[]{:S(2)}) %collective-permute-start.20) | collective-permute-done | bytes 65568 | tf_op jit(solution)/shard_map/ppermute | solution.py:544
  171.7 0.1 collective-permute-start.21
  171.8 4.3 %collective-permute-done.21 = f32[32,512]{1,0:T(8,128)S(1)} collective-permute-done((f32[32,512]{1,0:T(8,128)S(1)}, f32[32,512]{1,0:T(8,128)S(1)}, u32[]{:S(2)}, u32[]{:S(2)}) %collective-permute-start.21) | collective-permute-done | bytes 65568 | tf_op jit(solution)/shard_map/ppermute | solution.py:544
  176.1 5.7 %collective-permute-done.22 = f32[32,512]{1,0:T(8,128)S(1)} collective-permute-done((f32[32,512]{1,0:T(8,128)S(1)}, f32[32,512]{1,0:T(8,128)S(1)}, u32[]{:S(2)}, u32[]{:S(2)}) %collective-permute-start.22) | collective-permute-done | bytes 65568 | tf_op jit(solution)/shard_map/ppermute | solution.py:544
  181.9 0.1 collective-permute-start.23
  182.0 1.2 collective-permute-done.23.other_ref
  183.2 0.6 copy-done.10
  183.8 3.5 %later_weights.3.weights_ref = bf16[96,512]{1,0:T(8,128)(2,1)S(1)} custom-call(s32[1]{0:T(128)} %bitcast.bit_ref, f32[32,512]{1,0:T(8,128)} %copy-done.7, f32[32,512]{1,0:T(8,128)} %copy-done.10, f32[512,512]{1,0:T(8,128)} %copy-done.2), custom_call_target="tpu_custom_call" | custom-call | tf_op jit(solution)/shard_map/later_weights/pallas_call | solution.py:447
  187.3 7.9 %project_basis.1 = f32[32,16384]{1,0:T(8,128)} custom-call(bf16[96,512]{1,0:T(8,128)(2,1)S(1)} %later_weights.3.weights_ref, bf16[512,16384]{1,0:T(8,128)(2,1)} %get-tuple-element.13.fill_hbm), custom_call_target="tpu_custom_call" | custom-call | tf_op jit(solution)/shard_map/project_basis/pallas_call | solution.py:515
  (51 shorter events, 0.8 us)
Async XLA Ops:
  0.6 1.2 copy-start
  1.9 0.9 copy-start.3
  15.0 2.2 %collective-permute-start = (f32[256,640]{1,0:T(8,128)S(1)}, f32[256,640]{1,0:T(8,128)S(1)}, u32[]{:S(2)}, u32[]{:S(2)}) collective-permute-start(f32[256,640]{1,0:T(8,128)S(1)} %constant_dynamic-slice_fusion.8), channel_id=1, source_target_pairs={{0,4},{4,0},{8,12},{12,8},{16,20},{20,16},{24,28},{28,24},{1,5},{5... | collective-permute-start | bytes 1966088 | tf_op jit(solution)/shard_map/ppermute | solution.py:544
  17.3 40.7 %copy-start.1 = (bf16[32,16384]{1,0:T(8,128)(2,1)S(1)}, bf16[32,16384]{1,0:T(8,128)(2,1)}, u32[]{:S(2)}) copy-start(bf16[32,16384]{1,0:T(8,128)(2,1)} %basis_ref.3) | copy-start | bytes 3145732
  17.3 40.7 %copy-start.4 = (s32[512,128]{1,0:T(8,128)S(1)}, s32[512,128]{1,0:T(8,128)}, u32[]{:S(2)}) copy-start(s32[512,128]{1,0:T(8,128)} %flags_ref.3) | copy-start | bytes 786436
  17.4 8.0 %collective-permute-start.1 = (f32[128,640]{1,0:T(8,128)S(1)}, f32[128,640]{1,0:T(8,128)S(1)}, u32[]{:S(2)}, u32[]{:S(2)}) collective-permute-start(f32[128,640]{1,0:T(8,128)S(1)} %constant_dynamic-slice_fusion.7), channel_id=1, source_target_pairs={{0,8},{4,20},{8,0},{12,28},{16,24},{20,4},{24,16},{28,12},{1,9},{5... | collective-permute-start | bytes 983048 | tf_op jit(solution)/shard_map/ppermute | solution.py:544
  25.4 5.4 %collective-permute-start.2 = (f32[64,640]{1,0:T(8,128)S(1)}, f32[64,640]{1,0:T(8,128)S(1)}, u32[]{:S(2)}, u32[]{:S(2)}) collective-permute-start(f32[64,640]{1,0:T(8,128)S(1)} %constant_dynamic-slice_fusion.6), channel_id=1, source_target_pairs={{0,16},{4,12},{8,24},{12,4},{16,0},{20,28},{24,8},{28,20},{1,17},{... | collective-permute-start | bytes 491528 | tf_op jit(solution)/shard_map/ppermute | solution.py:544
  30.9 4.6 %collective-permute-start.3 = (f32[32,640]{1,0:T(8,128)S(1)}, f32[32,640]{1,0:T(8,128)S(1)}, u32[]{:S(2)}, u32[]{:S(2)}) collective-permute-start(f32[32,640]{1,0:T(8,128)S(1)} %constant_dynamic-slice_fusion.5), channel_id=1, source_target_pairs={{0,1},{1,0},{2,3},{3,2},{4,5},{5,4},{6,7},{7,6},{8,9},{9,8},{10,11... | collective-permute-start | bytes 245768 | tf_op jit(solution)/shard_map/ppermute | solution.py:544
  35.5 5.3 %collective-permute-start.4 = (f32[16,640]{1,0:T(8,128)S(1)}, f32[16,640]{1,0:T(8,128)S(1)}, u32[]{:S(2)}, u32[]{:S(2)}) collective-permute-start(f32[16,640]{1,0:T(8,128)S(1)} %constant_dynamic-slice_fusion.4), channel_id=1, source_target_pairs={{0,2},{1,3},{2,0},{3,1},{4,6},{5,7},{6,4},{7,5},{8,10},{9,11},{10,... | collective-permute-start | bytes 122888 | tf_op jit(solution)/shard_map/ppermute | solution.py:544
  44.0 13.9 %all-to-all-start = ((f32[32,4,128]{2,1,0:T(4,128)}), f32[32,4,128]{2,1,0:T(4,128)S(1)}, u32[]{:S(2)}, u32[]{:S(2)}) async-start(f32[32,4,128]{2,1,0:T(4,128)} %solve_share.1), calls=%async_computation | async-start | bytes 131072 | tf_op jit(solution)/shard_map/all_to_all | solution.py:609
  74.6 1.7 collective-permute-start.5
  74.7 31.2 %copy-start.9 = (s32[512,64]{0,1:T(8,128)S(1)}, s32[512,64]{0,1:T(8,128)}, u32[]{:S(2)}) copy-start(s32[512,64]{0,1:T(8,128)} %param.7) | copy-start | bytes 393220
  76.4 5.4 %collective-permute-start.6 = (f32[320,128]{1,0:T(8,128)S(1)}, f32[320,128]{1,0:T(8,128)S(1)}, u32[]{:S(2)}, u32[]{:S(2)}) collective-permute-start(f32[320,128]{1,0:T(8,128)S(1)} %constant_dynamic-slice_fusion.2), channel_id=1, source_target_pairs={{0,8},{4,20},{8,0},{12,28},{16,24},{20,4},{24,16},{28,12},{1,9},{5... | collective-permute-start | bytes 491528 | tf_op jit(solution)/shard_map/ppermute | solution.py:544
  81.8 5.4 %collective-permute-start.7 = (f32[320,128]{1,0:T(8,128)S(1)}, f32[320,128]{1,0:T(8,128)S(1)}, u32[]{:S(2)}, u32[]{:S(2)}) collective-permute-start(f32[320,128]{1,0:T(8,128)S(1)} %dynamic-slice_add_fusion.3), channel_id=1, source_target_pairs={{0,16},{4,12},{8,24},{12,4},{16,0},{20,28},{24,8},{28,20},{1,17},{... | collective-permute-start | bytes 491528 | tf_op jit(solution)/shard_map/ppermute | solution.py:544
  87.2 5.4 %collective-permute-start.8 = (f32[320,128]{1,0:T(8,128)S(1)}, f32[320,128]{1,0:T(8,128)S(1)}, u32[]{:S(2)}, u32[]{:S(2)}) collective-permute-start(f32[320,128]{1,0:T(8,128)S(1)} %add.131), channel_id=1, source_target_pairs={{0,1},{1,0},{2,3},{3,2},{4,5},{5,4},{6,7},{7,6},{8,9},{9,8},{10,11... | collective-permute-start | bytes 491528 | tf_op jit(solution)/shard_map/ppermute | solution.py:544
  92.6 7.7 %collective-permute-start.9 = (f32[320,128]{1,0:T(8,128)S(1)}, f32[320,128]{1,0:T(8,128)S(1)}, u32[]{:S(2)}, u32[]{:S(2)}) collective-permute-start(f32[320,128]{1,0:T(8,128)S(1)} %add.132), channel_id=1, source_target_pairs={{0,2},{1,3},{2,0},{3,1},{4,6},{5,7},{6,4},{7,5},{8,10},{9,11},{10,... | collective-permute-start | bytes 491528 | tf_op jit(solution)/shard_map/ppermute | solution.py:544
  100.3 5.4 %collective-permute-start.10 = (f32[320,128]{1,0:T(8,128)S(1)}, f32[320,128]{1,0:T(8,128)S(1)}, u32[]{:S(2)}, u32[]{:S(2)}) collective-permute-start(f32[320,128]{1,0:T(8,128)S(1)} %add.133), channel_id=1, source_target_pairs={{0,8},{4,20},{8,0},{12,28},{16,24},{20,4},{24,16},{28,12},{1,9},{5... | collective-permute-start | bytes 491528 | tf_op jit(solution)/shard_map/ppermute | solution.py:544
  105.8 1.7 copy-start.5
  105.8 1.7 collective-permute-start.11
  107.5 0.7 copy-start.6
  112.9 11.1 %copy-start.2 = (f32[512,512]{1,0:T(8,128)}, f32[512,512]{1,0:T(8,128)S(1)}, u32[]{:S(2)}) copy-start(f32[512,512]{1,0:T(8,128)S(1)} %get-tuple-element.14.full_ref) | copy-start | bytes 3145732
  124.1 1.3 collective-permute-start.12
  125.4 4.3 %collective-permute-start.13 = (f32[32,512]{1,0:T(8,128)S(1)}, f32[32,512]{1,0:T(8,128)S(1)}, u32[]{:S(2)}, u32[]{:S(2)}) collective-permute-start(f32[32,512]{1,0:T(8,128)S(1)} %dynamic-slice_add_fusion.7), channel_id=1, source_target_pairs={{0,8},{4,20},{8,0},{12,28},{16,24},{20,4},{24,16},{28,12},{1,9},{5... | collective-permute-start | bytes 196616 | tf_op jit(solution)/shard_map/ppermute | solution.py:544
  129.7 4.3 %collective-permute-start.14 = (f32[32,512]{1,0:T(8,128)S(1)}, f32[32,512]{1,0:T(8,128)S(1)}, u32[]{:S(2)}, u32[]{:S(2)}) collective-permute-start(f32[32,512]{1,0:T(8,128)S(1)} %add.137), channel_id=1, source_target_pairs={{0,16},{4,12},{8,24},{12,4},{16,0},{20,28},{24,8},{28,20},{1,17},{... | collective-permute-start | bytes 196616 | tf_op jit(solution)/shard_map/ppermute | solution.py:544
  134.1 4.3 %collective-permute-start.15 = (f32[32,512]{1,0:T(8,128)S(1)}, f32[32,512]{1,0:T(8,128)S(1)}, u32[]{:S(2)}, u32[]{:S(2)}) collective-permute-start(f32[32,512]{1,0:T(8,128)S(1)} %add.138), channel_id=1, source_target_pairs={{0,1},{1,0},{2,3},{3,2},{4,5},{5,4},{6,7},{7,6},{8,9},{9,8},{10,11... | collective-permute-start | bytes 196616 | tf_op jit(solution)/shard_map/ppermute | solution.py:544
  138.4 5.8 %collective-permute-start.16 = (f32[32,512]{1,0:T(8,128)S(1)}, f32[32,512]{1,0:T(8,128)S(1)}, u32[]{:S(2)}, u32[]{:S(2)}) collective-permute-start(f32[32,512]{1,0:T(8,128)S(1)} %add.139), channel_id=1, source_target_pairs={{0,2},{1,3},{2,0},{3,1},{4,6},{5,7},{6,4},{7,5},{8,10},{9,11},{10,... | collective-permute-start | bytes 196616 | tf_op jit(solution)/shard_map/ppermute | solution.py:544
  144.2 1.3 copy-start.8
  144.3 1.3 collective-permute-start.17
  145.6 0.6 copy-start.11
  161.7 1.3 collective-permute-start.18
  163.0 4.3 %collective-permute-start.19 = (f32[32,512]{1,0:T(8,128)S(1)}, f32[32,512]{1,0:T(8,128)S(1)}, u32[]{:S(2)}, u32[]{:S(2)}) collective-permute-start(f32[32,512]{1,0:T(8,128)S(1)} %dynamic-slice_add_fusion.6), channel_id=1, source_target_pairs={{0,8},{4,20},{8,0},{12,28},{16,24},{20,4},{24,16},{28,12},{1,9},{5... | collective-permute-start | bytes 196616 | tf_op jit(solution)/shard_map/ppermute | solution.py:544
  167.4 4.3 %collective-permute-start.20 = (f32[32,512]{1,0:T(8,128)S(1)}, f32[32,512]{1,0:T(8,128)S(1)}, u32[]{:S(2)}, u32[]{:S(2)}) collective-permute-start(f32[32,512]{1,0:T(8,128)S(1)} %add.142), channel_id=1, source_target_pairs={{0,16},{4,12},{8,24},{12,4},{16,0},{20,28},{24,8},{28,20},{1,17},{... | collective-permute-start | bytes 196616 | tf_op jit(solution)/shard_map/ppermute | solution.py:544
  171.7 4.3 %collective-permute-start.21 = (f32[32,512]{1,0:T(8,128)S(1)}, f32[32,512]{1,0:T(8,128)S(1)}, u32[]{:S(2)}, u32[]{:S(2)}) collective-permute-start(f32[32,512]{1,0:T(8,128)S(1)} %add.143), channel_id=1, source_target_pairs={{0,1},{1,0},{2,3},{3,2},{4,5},{5,4},{6,7},{7,6},{8,9},{9,8},{10,11... | collective-permute-start | bytes 196616 | tf_op jit(solution)/shard_map/ppermute | solution.py:544
  176.1 5.8 %collective-permute-start.22 = (f32[32,512]{1,0:T(8,128)S(1)}, f32[32,512]{1,0:T(8,128)S(1)}, u32[]{:S(2)}, u32[]{:S(2)}) collective-permute-start(f32[32,512]{1,0:T(8,128)S(1)} %add.144), channel_id=1, source_target_pairs={{0,2},{1,3},{2,0},{3,1},{4,6},{5,7},{6,4},{7,5},{8,10},{9,11},{10,... | collective-permute-start | bytes 196616 | tf_op jit(solution)/shard_map/ppermute | solution.py:544
  181.9 1.3 copy-start.7
  181.9 1.3 collective-permute-start.23
  183.2 0.6 copy-start.10

commit v3 on v2

--- a/solution.py
+++ b/solution.py
@@ -60,17 +60,20 @@
 
 def normal_kernel(
     chunk,
-    flags_ref,
+    flags_hbm,
     snap_hbm,
-    basis_ref,
+    basis_hbm,
     out_ref,
     masked_hbm,
+    flags_ref,
+    basis_ref,
     snap_ref,
     masked_ref,
     gram_ref,
     right_ref,
     arrived,
     left,
+    small,
 ):
     count, rows = snap_ref.shape
     modes = basis_ref.shape[0]
@@ -78,8 +81,14 @@
     blocks_step = chunk // LANES
     steps = rows // chunk
 
+    basis_copy = pltpu.make_async_copy(basis_hbm, basis_ref, small.at[0])
+    flags_copy = pltpu.make_async_copy(flags_hbm, flags_ref, small.at[1])
+    basis_copy.start()
+    flags_copy.start()
     fetch_all(snap_hbm, snap_ref, arrived, chunk)
     right_ref[...] = jnp.zeros_like(right_ref)
+    basis_copy.wait()
+    flags_copy.wait()
     all_flags = flags_ref[...].astype(F32)
 
     for block in range(rows // LANES):
@@ -144,26 +153,33 @@
     modes = basis.shape[0]
     blocks = flags.shape[1]
     width = modes * modes // 2 + LANES
-    whole = pl.BlockSpec(memory_space=pltpu.VMEM)
+    hbm = pl.BlockSpec(memory_space=pl.ANY)
     return pl.pallas_call(
         functools.partial(normal_kernel, chunk),
-        in_specs=[whole, pl.BlockSpec(memory_space=pl.ANY), whole],
-        out_specs=[whole, pl.BlockSpec(memory_space=pl.ANY)],
+        in_specs=[hbm] * 3,
+        out_specs=[pl.BlockSpec(memory_space=pltpu.VMEM), hbm],
         out_shape=[
             jax.ShapeDtypeStruct((count, width), F32),
             jax.ShapeDtypeStruct((count, rows), BF16),
         ],
         scratch_shapes=[
+            pltpu.VMEM((count, blocks), jnp.int32),
+            pltpu.VMEM((modes, rows), BF16),
             pltpu.VMEM((count, rows), BF16),
             pltpu.VMEM((count, rows), BF16),
             pltpu.VMEM((blocks * modes, LANES), F32),
             pltpu.VMEM((count, modes), F32),
             pltpu.SemaphoreType.DMA((rows // chunk,)),
             pltpu.SemaphoreType.DMA((rows // chunk,)),
+            pltpu.SemaphoreType.DMA((2,)),
         ],
         compiler_params=pltpu.CompilerParams(vmem_limit_bytes=SCRATCH_BYTES),
         name="normal_terms",
-    )(flags, snapshots, basis)
+    )(
+        pltpu.with_memory_space_constraint(flags, pltpu.HBM),
+        snapshots,
+        pltpu.with_memory_space_constraint(basis, pltpu.HBM),
+    )
 
 
 def solve_kernel(modes, shift, in_ref, out_ref, turned_ref, system_ref):

time: 196 us -> 198 us (1.010)
  Pallas kernels: 74 us -> 78.9 us
  local copies, waits for them, and re-layouts: 5.23 us -> 3.05 us
    pallas_call x1, Pallas kernels: 12.1 us -> 17.1 us  [normal_terms(): pl.pallas_call(functools.partial(normal_kernel, chunk), in_specs=[hbm] *...]
    unnamed x25 -> x21, local copies, waits for them, and re-layouts: 5 us -> 2.83 us
where the time goes in v3:
time: 198 us
  waiting for transfers between devices  89.3 us (45%)
  Pallas kernels  78.9 us (40%)
  starting transfers between devices  24.6 us (12%)
  local copies, waits for them, and re-layouts  3.05 us (2%)
    ppermute x24, waiting for transfers between devices, swap(): return lax.ppermute(values, self.axis, self.pairs)  82 us
    pallas_call x2, Pallas kernels, next_mixer(): pl.pallas_call(functools.partial(mixer_kernel, chunk), in_specs=[whole, p...  21.8 us
    ppermute x24, starting transfers between devices, swap(): return lax.ppermute(values, self.axis, self.pairs)  18 us
    pallas_call x1, Pallas kernels, normal_terms(): pl.pallas_call(functools.partial(normal_kernel, chunk), in_specs=[hbm] *...  17.1 us
    pallas_call x1, Pallas kernels, refill_correlate(): pl.pallas_call(functools.partial(refill_kernel, chunk, order), in_specs=[...  16.6 us
    pallas_call x2, Pallas kernels, later_weights(): pl.pallas_call(functools.partial(later_kernel, rows, scale), in_specs=wei...  8.21 us
    pallas_call x1, Pallas kernels, project_basis(): pl.pallas_call(functools.partial(basis_kernel, chunk), in_specs=[pl.Block...  7.9 us
    all_to_all x1, waiting for transfers between devices, per_device(): shares = lax.all_to_all(shares, AXES, 0, 0, tiled=True)  7.32 us
  transfers between devices with their start and end apart: 25, of which 25 were waited for; matrix products, arithmetic and copies ran while one was open for 0% of the time, Pallas kernels for 0%

profile of v3, /device:TPU:0, one launch (start us, length us, event | category | flops | bytes accessed | tf_op | source)
XLA Modules:
  0.0 198.1 jit_solution(13649227459293738924)
XLA Ops:
  0.6 17.1 %normal_terms.1 = (f32[512,640]{1,0:T(8,128)S(1)}, bf16[512,16384]{1,0:T(8,128)(2,1)}) custom-call(s32[512,128]{1,0:T(8,128)} %flags_ref.1, bf16[512,16384]{1,0:T(8,128)(2,1)} %snap_hbm.1, bf16[32,16384]{1,0:T(8,128)(2,1)} %basis_ref.1), custom_call_target="tpu_custom_call" | custom-call | tf_op jit(solution)/shard_map/normal_terms/pallas_call | solution.py:157
  17.8 0.5 collective-permute-start
  18.3 1.7 collective-permute-done
  20.1 2.9 %collective-permute-start.1 = (f32[128,640]{1,0:T(8,128)S(1)}, f32[128,640]{1,0:T(8,128)S(1)}, u32[]{:S(2)}, u32[]{:S(2)}) collective-permute-start(f32[128,640]{1,0:T(8,128)S(1)} %constant_dynamic-slice_fusion.7), channel_id=1, source_target_pairs={{0,8},{4,20},{8,0},{12,28},{16,24},{20,4},{24,16},{28,12},{1,9},{5... | collective-permute-start | bytes 983048 | tf_op jit(solution)/shard_map/ppermute | solution.py:560
  23.1 5.1 %collective-permute-done.1 = f32[128,640]{1,0:T(8,128)S(1)} collective-permute-done((f32[128,640]{1,0:T(8,128)S(1)}, f32[128,640]{1,0:T(8,128)S(1)}, u32[]{:S(2)}, u32[]{:S(2)}) %collective-permute-start.1) | collective-permute-done | bytes 327712 | tf_op jit(solution)/shard_map/ppermute | solution.py:560
  28.2 2.1 %collective-permute-start.2 = (f32[64,640]{1,0:T(8,128)S(1)}, f32[64,640]{1,0:T(8,128)S(1)}, u32[]{:S(2)}, u32[]{:S(2)}) collective-permute-start(f32[64,640]{1,0:T(8,128)S(1)} %constant_dynamic-slice_fusion.6), channel_id=1, source_target_pairs={{0,16},{4,12},{8,24},{12,4},{16,0},{20,28},{24,8},{28,20},{1,17},{... | collective-permute-start | bytes 491528 | tf_op jit(solution)/shard_map/ppermute | solution.py:560
  30.3 3.3 %collective-permute-done.2 = f32[64,640]{1,0:T(8,128)S(1)} collective-permute-done((f32[64,640]{1,0:T(8,128)S(1)}, f32[64,640]{1,0:T(8,128)S(1)}, u32[]{:S(2)}, u32[]{:S(2)}) %collective-permute-start.2) | collective-permute-done | bytes 163872 | tf_op jit(solution)/shard_map/ppermute | solution.py:560
  33.6 2.1 %collective-permute-start.3 = (f32[32,640]{1,0:T(8,128)S(1)}, f32[32,640]{1,0:T(8,128)S(1)}, u32[]{:S(2)}, u32[]{:S(2)}) collective-permute-start(f32[32,640]{1,0:T(8,128)S(1)} %constant_dynamic-slice_fusion.5), channel_id=1, source_target_pairs={{0,1},{1,0},{2,3},{3,2},{4,5},{5,4},{6,7},{7,6},{8,9},{9,8},{10,11... | collective-permute-start | bytes 245768 | tf_op jit(solution)/shard_map/ppermute | solution.py:560
  35.8 2.4 %collective-permute-done.3 = f32[32,640]{1,0:T(8,128)S(1)} collective-permute-done((f32[32,640]{1,0:T(8,128)S(1)}, f32[32,640]{1,0:T(8,128)S(1)}, u32[]{:S(2)}, u32[]{:S(2)}) %collective-permute-start.3) | collective-permute-done | bytes 81952 | tf_op jit(solution)/shard_map/ppermute | solution.py:560
  38.3 3.3 %collective-permute-start.4 = (f32[16,640]{1,0:T(8,128)S(1)}, f32[16,640]{1,0:T(8,128)S(1)}, u32[]{:S(2)}, u32[]{:S(2)}) collective-permute-start(f32[16,640]{1,0:T(8,128)S(1)} %constant_dynamic-slice_fusion.4), channel_id=1, source_target_pairs={{0,2},{1,3},{2,0},{3,1},{4,6},{5,7},{6,4},{7,5},{8,10},{9,11},{10,... | collective-permute-start | bytes 122888 | tf_op jit(solution)/shard_map/ppermute | solution.py:560
  41.5 2.0 %collective-permute-done.4 = f32[16,640]{1,0:T(8,128)S(1)} collective-permute-done((f32[16,640]{1,0:T(8,128)S(1)}, f32[16,640]{1,0:T(8,128)S(1)}, u32[]{:S(2)}, u32[]{:S(2)}) %collective-permute-start.4) | collective-permute-done | bytes 40992 | tf_op jit(solution)/shard_map/ppermute | solution.py:560
  43.5 0.6 dynamic-slice_add_fusion.8.in_ref
  44.1 2.7 %solve_share.1 = f32[32,4,128]{2,1,0:T(4,128)} custom-call(f32[16,640]{1,0:T(8,128)} %dynamic-slice_add_fusion.8.in_ref), custom_call_target="tpu_custom_call" | custom-call | tf_op jit(solution)/shard_map/solve_share/pallas_call | solution.py:233
  46.8 6.6 %all-to-all-start = ((f32[32,4,128]{2,1,0:T(4,128)}), f32[32,4,128]{2,1,0:T(4,128)S(1)}, u32[]{:S(2)}, u32[]{:S(2)}) async-start(f32[32,4,128]{2,1,0:T(4,128)} %solve_share.1), calls=%async_computation | async-start | bytes 131072 | tf_op jit(solution)/shard_map/all_to_all | solution.py:625
  53.4 7.3 %all-to-all-done.shares_ref = f32[32,4,128]{2,1,0:T(4,128)S(1)} async-done(((f32[32,4,128]{2,1,0:T(4,128)}), f32[32,4,128]{2,1,0:T(4,128)S(1)}, u32[]{:S(2)}, u32[]{:S(2)}) %all-to-all-start) | async-done | bytes 65568 | tf_op jit(solution)/shard_map/all_to_all | solution.py:625
  60.8 16.6 %refill_correlate.1 = (bf16[512,16384]{1,0:T(8,128)(2,1)}, f32[1280,128]{1,0:T(8,128)S(1)}, f32[32,512]{1,0:T(8,128)}) custom-call(s32[512,128]{1,0:T(8,128)S(1)} %copy-done.2, bf16[512,16384]{1,0:T(8,128)(2,1)} %get-tuple-element.9.masked_hbm, bf16[32,16384]{1,0:T(8,128)(2,1)S(1)} %copy-done, f32[32,4,128]{2,1,0:T(4,128)S(1)} %all-to-all-done.shares_ref), custom_call_target="tpu_custom_call" | custom-call | tf_op jit(solution)/shard_map/refill_correlate/pallas_call | solution.py:343
  77.4 0.1 collective-permute-start.5
  77.5 1.6 collective-permute-done.5
  79.1 0.7 collective-permute-start.6
  79.9 4.7 %collective-permute-done.6 = f32[320,128]{1,0:T(8,128)S(1)} collective-permute-done((f32[320,128]{1,0:T(8,128)S(1)}, f32[320,128]{1,0:T(8,128)S(1)}, u32[]{:S(2)}, u32[]{:S(2)}) %collective-permute-start.6) | collective-permute-done | bytes 163872 | tf_op jit(solution)/shard_map/ppermute | solution.py:560
  84.6 0.7 collective-permute-start.7
  85.3 4.6 %collective-permute-done.7 = f32[320,128]{1,0:T(8,128)S(1)} collective-permute-done((f32[320,128]{1,0:T(8,128)S(1)}, f32[320,128]{1,0:T(8,128)S(1)}, u32[]{:S(2)}, u32[]{:S(2)}) %collective-permute-start.7) | collective-permute-done | bytes 163872 | tf_op jit(solution)/shard_map/ppermute | solution.py:560
  90.0 0.3 collective-permute-start.8
  90.3 5.1 %collective-permute-done.8 = f32[320,128]{1,0:T(8,128)S(1)} collective-permute-done((f32[320,128]{1,0:T(8,128)S(1)}, f32[320,128]{1,0:T(8,128)S(1)}, u32[]{:S(2)}, u32[]{:S(2)}) %collective-permute-start.8) | collective-permute-done | bytes 163872 | tf_op jit(solution)/shard_map/ppermute | solution.py:560
  95.4 0.5 collective-permute-start.9
  95.9 7.2 %collective-permute-done.9 = f32[320,128]{1,0:T(8,128)S(1)} collective-permute-done((f32[320,128]{1,0:T(8,128)S(1)}, f32[320,128]{1,0:T(8,128)S(1)}, u32[]{:S(2)}, u32[]{:S(2)}) %collective-permute-start.9) | collective-permute-done | bytes 163872 | tf_op jit(solution)/shard_map/ppermute | solution.py:560
  103.1 0.7 collective-permute-start.10
  103.8 4.6 %collective-permute-done.10 = f32[320,128]{1,0:T(8,128)S(1)} collective-permute-done((f32[320,128]{1,0:T(8,128)S(1)}, f32[320,128]{1,0:T(8,128)S(1)}, u32[]{:S(2)}, u32[]{:S(2)}) %collective-permute-start.10) | collective-permute-done | bytes 163872 | tf_op jit(solution)/shard_map/ppermute | solution.py:560
  108.6 0.1 collective-permute-start.11
  108.6 0.8 copy.6.seed_ref
  109.5 0.8 collective-permute-done.11.other_ref
  110.3 0.7 copy-done.4
  111.0 4.7 %first_weights.1 = (bf16[192,512]{1,0:T(8,128)(2,1)S(1)}, f32[512,512]{1,0:T(8,128)S(1)}) custom-call(s32[1]{0:T(128)} %bitcast.bit_ref, f32[640,128]{1,0:T(8,128)} %copy-done.3, f32[640,128]{1,0:T(8,128)} %copy-done.4, s32[512,64]{1,0:T(8,128)} %copy.6.seed_ref), custom_call_target="tpu_custom_call" | custom-call | tf_op jit(solution)/shard_map/first_weights/pallas_call | solution.py:451
  115.7 11.1 %next_mixer.2 = f32[64,512]{1,0:T(8,128)S(1)} custom-call(bf16[192,512]{1,0:T(8,128)(2,1)S(1)} %get-tuple-element.12.weights_ref, bf16[512,16384]{1,0:T(8,128)(2,1)} %get-tuple-element.13.fill_hbm), custom_call_target="tpu_custom_call" | custom-call | tf_op jit(solution)/shard_map/next_mixer/pallas_call | solution.py:492
  126.8 0.2 collective-permute-start.12
  127.0 1.1 collective-permute-done.12
  128.2 0.7 collective-permute-start.13
  128.9 3.6 %collective-permute-done.13 = f32[32,512]{1,0:T(8,128)S(1)} collective-permute-done((f32[32,512]{1,0:T(8,128)S(1)}, f32[32,512]{1,0:T(8,128)S(1)}, u32[]{:S(2)}, u32[]{:S(2)}) %collective-permute-start.13) | collective-permute-done | bytes 65568 | tf_op jit(solution)/shard_map/ppermute | solution.py:560
  132.5 0.8 collective-permute-start.14
  133.3 3.6 %collective-permute-done.14 = f32[32,512]{1,0:T(8,128)S(1)} collective-permute-done((f32[32,512]{1,0:T(8,128)S(1)}, f32[32,512]{1,0:T(8,128)S(1)}, u32[]{:S(2)}, u32[]{:S(2)}) %collective-permute-start.14) | collective-permute-done | bytes 65568 | tf_op jit(solution)/shard_map/ppermute | solution.py:560
  136.8 0.1 collective-permute-start.15
  136.9 4.3 %collective-permute-done.15 = f32[32,512]{1,0:T(8,128)S(1)} collective-permute-done((f32[32,512]{1,0:T(8,128)S(1)}, f32[32,512]{1,0:T(8,128)S(1)}, u32[]{:S(2)}, u32[]{:S(2)}) %collective-permute-start.15) | collective-permute-done | bytes 65568 | tf_op jit(solution)/shard_map/ppermute | solution.py:560
  141.2 0.1 collective-permute-start.16
  141.3 5.7 %collective-permute-done.16 = f32[32,512]{1,0:T(8,128)S(1)} collective-permute-done((f32[32,512]{1,0:T(8,128)S(1)}, f32[32,512]{1,0:T(8,128)S(1)}, u32[]{:S(2)}, u32[]{:S(2)}) %collective-permute-start.16) | collective-permute-done | bytes 65568 | tf_op jit(solution)/shard_map/ppermute | solution.py:560
  147.0 0.1 collective-permute-start.17
  147.1 1.2 collective-permute-done.17.other_ref
  148.3 0.6 copy-done.9
  149.0 4.8 %later_weights.2.weights_ref = bf16[192,512]{1,0:T(8,128)(2,1)S(1)} custom-call(s32[1]{0:T(128)} %bitcast.bit_ref, f32[32,512]{1,0:T(8,128)} %copy-done.6, f32[32,512]{1,0:T(8,128)} %copy-done.9, f32[512,512]{1,0:T(8,128)} %copy-done.1), custom_call_target="tpu_custom_call" | custom-call | tf_op jit(solution)/shard_map/later_weights/pallas_call | solution.py:463
  153.7 10.7 %next_mixer.3 = f32[64,512]{1,0:T(8,128)S(1)} custom-call(bf16[192,512]{1,0:T(8,128)(2,1)S(1)} %later_weights.2.weights_ref, bf16[512,16384]{1,0:T(8,128)(2,1)} %get-tuple-element.13.fill_hbm), custom_call_target="tpu_custom_call" | custom-call | tf_op jit(solution)/shard_map/next_mixer/pallas_call | solution.py:492
  164.5 0.2 collective-permute-start.18
  164.7 1.1 collective-permute-done.18
  165.8 0.7 collective-permute-start.19
  166.5 3.6 %collective-permute-done.19 = f32[32,512]{1,0:T(8,128)S(1)} collective-permute-done((f32[32,512]{1,0:T(8,128)S(1)}, f32[32,512]{1,0:T(8,128)S(1)}, u32[]{:S(2)}, u32[]{:S(2)}) %collective-permute-start.19) | collective-permute-done | bytes 65568 | tf_op jit(solution)/shard_map/ppermute | solution.py:560
  170.1 0.8 collective-permute-start.20
  170.9 3.6 %collective-permute-done.20 = f32[32,512]{1,0:T(8,128)S(1)} collective-permute-done((f32[32,512]{1,0:T(8,128)S(1)}, f32[32,512]{1,0:T(8,128)S(1)}, u32[]{:S(2)}, u32[]{:S(2)}) %collective-permute-start.20) | collective-permute-done | bytes 65568 | tf_op jit(solution)/shard_map/ppermute | solution.py:560
  174.5 0.1 collective-permute-start.21
  174.6 4.3 %collective-permute-done.21 = f32[32,512]{1,0:T(8,128)S(1)} collective-permute-done((f32[32,512]{1,0:T(8,128)S(1)}, f32[32,512]{1,0:T(8,128)S(1)}, u32[]{:S(2)}, u32[]{:S(2)}) %collective-permute-start.21) | collective-permute-done | bytes 65568 | tf_op jit(solution)/shard_map/ppermute | solution.py:560
  178.8 0.1 collective-permute-start.22
  178.9 5.7 %collective-permute-done.22 = f32[32,512]{1,0:T(8,128)S(1)} collective-permute-done((f32[32,512]{1,0:T(8,128)S(1)}, f32[32,512]{1,0:T(8,128)S(1)}, u32[]{:S(2)}, u32[]{:S(2)}) %collective-permute-start.22) | collective-permute-done | bytes 65568 | tf_op jit(solution)/shard_map/ppermute | solution.py:560
  184.7 0.1 collective-permute-start.23
  184.7 1.2 collective-permute-done.23.other_ref
  186.0 0.6 copy-done.8
  186.6 3.5 %later_weights.3.weights_ref = bf16[96,512]{1,0:T(8,128)(2,1)S(1)} custom-call(s32[1]{0:T(128)} %bitcast.bit_ref, f32[32,512]{1,0:T(8,128)} %copy-done.5, f32[32,512]{1,0:T(8,128)} %copy-done.8, f32[512,512]{1,0:T(8,128)} %copy-done.1), custom_call_target="tpu_custom_call" | custom-call | tf_op jit(solution)/shard_map/later_weights/pallas_call | solution.py:463
  190.1 7.9 %project_basis.1 = f32[32,16384]{1,0:T(8,128)} custom-call(bf16[96,512]{1,0:T(8,128)(2,1)S(1)} %later_weights.3.weights_ref, bf16[512,16384]{1,0:T(8,128)(2,1)} %get-tuple-element.13.fill_hbm), custom_call_target="tpu_custom_call" | custom-call | tf_op jit(solution)/shard_map/project_basis/pallas_call | solution.py:531
  (47 shorter events, 0.7 us)
Async XLA Ops:
  17.8 2.2 %collective-permute-start = (f32[256,640]{1,0:T(8,128)S(1)}, f32[256,640]{1,0:T(8,128)S(1)}, u32[]{:S(2)}, u32[]{:S(2)}) collective-permute-start(f32[256,640]{1,0:T(8,128)S(1)} %constant_dynamic-slice_fusion.8), channel_id=1, source_target_pairs={{0,4},{4,0},{8,12},{12,8},{16,20},{20,16},{24,28},{28,24},{1,5},{5... | collective-permute-start | bytes 1966088 | tf_op jit(solution)/shard_map/ppermute | solution.py:560
  20.1 40.7 %copy-start = (bf16[32,16384]{1,0:T(8,128)(2,1)S(1)}, bf16[32,16384]{1,0:T(8,128)(2,1)}, u32[]{:S(2)}) copy-start(bf16[32,16384]{1,0:T(8,128)(2,1)} %basis_ref.1) | copy-start | bytes 3145732
  20.1 40.7 %copy-start.2 = (s32[512,128]{1,0:T(8,128)S(1)}, s32[512,128]{1,0:T(8,128)}, u32[]{:S(2)}) copy-start(s32[512,128]{1,0:T(8,128)} %flags_ref.1) | copy-start | bytes 786436
  20.1 8.0 %collective-permute-start.1 = (f32[128,640]{1,0:T(8,128)S(1)}, f32[128,640]{1,0:T(8,128)S(1)}, u32[]{:S(2)}, u32[]{:S(2)}) collective-permute-start(f32[128,640]{1,0:T(8,128)S(1)} %constant_dynamic-slice_fusion.7), channel_id=1, source_target_pairs={{0,8},{4,20},{8,0},{12,28},{16,24},{20,4},{24,16},{28,12},{1,9},{5... | collective-permute-start | bytes 983048 | tf_op jit(solution)/shard_map/ppermute | solution.py:560
  28.2 5.4 %collective-permute-start.2 = (f32[64,640]{1,0:T(8,128)S(1)}, f32[64,640]{1,0:T(8,128)S(1)}, u32[]{:S(2)}, u32[]{:S(2)}) collective-permute-start(f32[64,640]{1,0:T(8,128)S(1)} %constant_dynamic-slice_fusion.6), channel_id=1, source_target_pairs={{0,16},{4,12},{8,24},{12,4},{16,0},{20,28},{24,8},{28,20},{1,17},{... | collective-permute-start | bytes 491528 | tf_op jit(solution)/shard_map/ppermute | solution.py:560
  33.6 4.6 %collective-permute-start.3 = (f32[32,640]{1,0:T(8,128)S(1)}, f32[32,640]{1,0:T(8,128)S(1)}, u32[]{:S(2)}, u32[]{:S(2)}) collective-permute-start(f32[32,640]{1,0:T(8,128)S(1)} %constant_dynamic-slice_fusion.5), channel_id=1, source_target_pairs={{0,1},{1,0},{2,3},{3,2},{4,5},{5,4},{6,7},{7,6},{8,9},{9,8},{10,11... | collective-permute-start | bytes 245768 | tf_op jit(solution)/shard_map/ppermute | solution.py:560
  38.3 5.3 %collective-permute-start.4 = (f32[16,640]{1,0:T(8,128)S(1)}, f32[16,640]{1,0:T(8,128)S(1)}, u32[]{:S(2)}, u32[]{:S(2)}) collective-permute-start(f32[16,640]{1,0:T(8,128)S(1)} %constant_dynamic-slice_fusion.4), channel_id=1, source_target_pairs={{0,2},{1,3},{2,0},{3,1},{4,6},{5,7},{6,4},{7,5},{8,10},{9,11},{10,... | collective-permute-start | bytes 122888 | tf_op jit(solution)/shard_map/ppermute | solution.py:560
  46.8 13.9 %all-to-all-start = ((f32[32,4,128]{2,1,0:T(4,128)}), f32[32,4,128]{2,1,0:T(4,128)S(1)}, u32[]{:S(2)}, u32[]{:S(2)}) async-start(f32[32,4,128]{2,1,0:T(4,128)} %solve_share.1), calls=%async_computation | async-start | bytes 131072 | tf_op jit(solution)/shard_map/all_to_all | solution.py:625
  77.4 1.7 collective-permute-start.5
  77.5 31.2 %copy-start.7 = (s32[512,64]{0,1:T(8,128)S(1)}, s32[512,64]{0,1:T(8,128)}, u32[]{:S(2)}) copy-start(s32[512,64]{0,1:T(8,128)} %param.7) | copy-start | bytes 393220
  79.1 5.4 %collective-permute-start.6 = (f32[320,128]{1,0:T(8,128)S(1)}, f32[320,128]{1,0:T(8,128)S(1)}, u32[]{:S(2)}, u32[]{:S(2)}) collective-permute-start(f32[320,128]{1,0:T(8,128)S(1)} %constant_dynamic-slice_fusion.2), channel_id=1, source_target_pairs={{0,8},{4,20},{8,0},{12,28},{16,24},{20,4},{24,16},{28,12},{1,9},{5... | collective-permute-start | bytes 491528 | tf_op jit(solution)/shard_map/ppermute | solution.py:560
  84.6 5.4 %collective-permute-start.7 = (f32[320,128]{1,0:T(8,128)S(1)}, f32[320,128]{1,0:T(8,128)S(1)}, u32[]{:S(2)}, u32[]{:S(2)}) collective-permute-start(f32[320,128]{1,0:T(8,128)S(1)} %dynamic-slice_add_fusion.3), channel_id=1, source_target_pairs={{0,16},{4,12},{8,24},{12,4},{16,0},{20,28},{24,8},{28,20},{1,17},{... | collective-permute-start | bytes 491528 | tf_op jit(solution)/shard_map/ppermute | solution.py:560
  90.0 5.4 %collective-permute-start.8 = (f32[320,128]{1,0:T(8,128)S(1)}, f32[320,128]{1,0:T(8,128)S(1)}, u32[]{:S(2)}, u32[]{:S(2)}) collective-permute-start(f32[320,128]{1,0:T(8,128)S(1)} %add.131), channel_id=1, source_target_pairs={{0,1},{1,0},{2,3},{3,2},{4,5},{5,4},{6,7},{7,6},{8,9},{9,8},{10,11... | collective-permute-start | bytes 491528 | tf_op jit(solution)/shard_map/ppermute | solution.py:560
  95.4 7.7 %collective-permute-start.9 = (f32[320,128]{1,0:T(8,128)S(1)}, f32[320,128]{1,0:T(8,128)S(1)}, u32[]{:S(2)}, u32[]{:S(2)}) collective-permute-start(f32[320,128]{1,0:T(8,128)S(1)} %add.132), channel_id=1, source_target_pairs={{0,2},{1,3},{2,0},{3,1},{4,6},{5,7},{6,4},{7,5},{8,10},{9,11},{10,... | collective-permute-start | bytes 491528 | tf_op jit(solution)/shard_map/ppermute | solution.py:560
  103.1 5.4 %collective-permute-start.10 = (f32[320,128]{1,0:T(8,128)S(1)}, f32[320,128]{1,0:T(8,128)S(1)}, u32[]{:S(2)}, u32[]{:S(2)}) collective-permute-start(f32[320,128]{1,0:T(8,128)S(1)} %add.133), channel_id=1, source_target_pairs={{0,8},{4,20},{8,0},{12,28},{16,24},{20,4},{24,16},{28,12},{1,9},{5... | collective-permute-start | bytes 491528 | tf_op jit(solution)/shard_map/ppermute | solution.py:560
  108.5 1.7 copy-start.3
  108.6 1.7 collective-permute-start.11
  110.2 0.7 copy-start.4
  115.7 11.1 %copy-start.1 = (f32[512,512]{1,0:T(8,128)}, f32[512,512]{1,0:T(8,128)S(1)}, u32[]{:S(2)}) copy-start(f32[512,512]{1,0:T(8,128)S(1)} %get-tuple-element.14.full_ref) | copy-start | bytes 3145732
  126.8 1.3 collective-permute-start.12
  128.2 4.3 %collective-permute-start.13 = (f32[32,512]{1,0:T(8,128)S(1)}, f32[32,512]{1,0:T(8,128)S(1)}, u32[]{:S(2)}, u32[]{:S(2)}) collective-permute-start(f32[32,512]{1,0:T(8,128)S(1)} %dynamic-slice_add_fusion.7), channel_id=1, source_target_pairs={{0,8},{4,20},{8,0},{12,28},{16,24},{20,4},{24,16},{28,12},{1,9},{5... | collective-permute-start | bytes 196616 | tf_op jit(solution)/shard_map/ppermute | solution.py:560
  132.5 4.3 %collective-permute-start.14 = (f32[32,512]{1,0:T(8,128)S(1)}, f32[32,512]{1,0:T(8,128)S(1)}, u32[]{:S(2)}, u32[]{:S(2)}) collective-permute-start(f32[32,512]{1,0:T(8,128)S(1)} %add.137), channel_id=1, source_target_pairs={{0,16},{4,12},{8,24},{12,4},{16,0},{20,28},{24,8},{28,20},{1,17},{... | collective-permute-start | bytes 196616 | tf_op jit(solution)/shard_map/ppermute | solution.py:560
  136.8 4.3 %collective-permute-start.15 = (f32[32,512]{1,0:T(8,128)S(1)}, f32[32,512]{1,0:T(8,128)S(1)}, u32[]{:S(2)}, u32[]{:S(2)}) collective-permute-start(f32[32,512]{1,0:T(8,128)S(1)} %add.138), channel_id=1, source_target_pairs={{0,1},{1,0},{2,3},{3,2},{4,5},{5,4},{6,7},{7,6},{8,9},{9,8},{10,11... | collective-permute-start | bytes 196616 | tf_op jit(solution)/shard_map/ppermute | solution.py:560
  141.2 5.8 %collective-permute-start.16 = (f32[32,512]{1,0:T(8,128)S(1)}, f32[32,512]{1,0:T(8,128)S(1)}, u32[]{:S(2)}, u32[]{:S(2)}) collective-permute-start(f32[32,512]{1,0:T(8,128)S(1)} %add.139), channel_id=1, source_target_pairs={{0,2},{1,3},{2,0},{3,1},{4,6},{5,7},{6,4},{7,5},{8,10},{9,11},{10,... | collective-permute-start | bytes 196616 | tf_op jit(solution)/shard_map/ppermute | solution.py:560
  147.0 1.3 copy-start.6
  147.0 1.3 collective-permute-start.17
  148.3 0.6 copy-start.9
  164.5 1.3 collective-permute-start.18
  165.8 4.3 %collective-permute-start.19 = (f32[32,512]{1,0:T(8,128)S(1)}, f32[32,512]{1,0:T(8,128)S(1)}, u32[]{:S(2)}, u32[]{:S(2)}) collective-permute-start(f32[32,512]{1,0:T(8,128)S(1)} %dynamic-slice_add_fusion.6), channel_id=1, source_target_pairs={{0,8},{4,20},{8,0},{12,28},{16,24},{20,4},{24,16},{28,12},{1,9},{5... | collective-permute-start | bytes 196616 | tf_op jit(solution)/shard_map/ppermute | solution.py:560
  170.1 4.3 %collective-permute-start.20 = (f32[32,512]{1,0:T(8,128)S(1)}, f32[32,512]{1,0:T(8,128)S(1)}, u32[]{:S(2)}, u32[]{:S(2)}) collective-permute-start(f32[32,512]{1,0:T(8,128)S(1)} %add.142), channel_id=1, source_target_pairs={{0,16},{4,12},{8,24},{12,4},{16,0},{20,28},{24,8},{28,20},{1,17},{... | collective-permute-start | bytes 196616 | tf_op jit(solution)/shard_map/ppermute | solution.py:560
  174.5 4.3 %collective-permute-start.21 = (f32[32,512]{1,0:T(8,128)S(1)}, f32[32,512]{1,0:T(8,128)S(1)}, u32[]{:S(2)}, u32[]{:S(2)}) collective-permute-start(f32[32,512]{1,0:T(8,128)S(1)} %add.143), channel_id=1, source_target_pairs={{0,1},{1,0},{2,3},{3,2},{4,5},{5,4},{6,7},{7,6},{8,9},{9,8},{10,11... | collective-permute-start | bytes 196616 | tf_op jit(solution)/shard_map/ppermute | solution.py:560
  178.8 5.8 %collective-permute-start.22 = (f32[32,512]{1,0:T(8,128)S(1)}, f32[32,512]{1,0:T(8,128)S(1)}, u32[]{:S(2)}, u32[]{:S(2)}) collective-permute-start(f32[32,512]{1,0:T(8,128)S(1)} %add.144), channel_id=1, source_target_pairs={{0,2},{1,3},{2,0},{3,1},{4,6},{5,7},{6,4},{7,5},{8,10},{9,11},{10,... | collective-permute-start | bytes 196616 | tf_op jit(solution)/shard_map/ppermute | solution.py:560
  184.6 1.3 copy-start.5
  184.7 1.3 collective-permute-start.23
  186.0 0.6 copy-start.8
